TPU v7x, 512 devices: a whole 4x4x16 slice. The times are simulated.
512 devices in a mesh: expert: 32 (over z, core), fsdp: 16 (over y, x).
Axes of the slice: x: 4, y: 4, z: 16, core: 2. Of those that a mesh axis runs over, the one named last changes fastest.
Arguments:
- states: bfloat16 [65536, 512], P(('expert', 'fsdp')), may hold values from -6 to 6
- rates: bfloat16 [65536, 512], P(('expert', 'fsdp')), may hold values from -6 to 6
- expert_ids: int32 [65536, 2], P(('expert', 'fsdp')), may hold values from 0 to 63, all different within a row; in each aligned block of 128 rows (0 to 127, 128 to 255, ...) at most 8 rows name the same one
- gate_weights: float32 [65536, 2], P(('expert', 'fsdp')), may hold values from 0.25 to 1
- cotangent: bfloat16 [65536, 512], P(('expert', 'fsdp')), may hold values from -6 to 6
- weight_in: bfloat16 [512, 64, 1024], P('fsdp', 'expert'), may hold values from -0.25 to 0.25
- weight_out: bfloat16 [1024, 64, 512], P('fsdp', 'expert'), may hold values from -0.1875 to 0.1875
Outputs:
- defect: bfloat16 [65536, 512], P(('expert', 'fsdp'))
- grad_states: bfloat16 [65536, 512], P(('expert', 'fsdp'))
- grad_in: bfloat16 [512, 64, 1024], P('fsdp', 'expert')
- grad_out: bfloat16 [1024, 64, 512], P('fsdp', 'expert')
Inputs may be any that keep to these rules, and one draw needn't show every extreme that they name: `expert_ids`: A knot's two ids differ. Within each aligned block of 128 knots (the knots of one device) no expert is named by more than 8 of the block's entries, a bound that some block reaches.
All inputs are finite; a program needn't handle non-finite values.
Results may differ from a plain program's by a relative error of at most 0.019.
Values may be sent and summed in bfloat16 or wider, within the bound.
No kernel may reach another device: no remote copies, remote signals or barrier semaphores. Data moves between devices by JAX's collectives and lax.ppermute only.
A program may use at most 64 MiB of HBM per device.

v0:
```python
import jax
import jax.numpy as jnp
from jax import lax
from jax.sharding import PartitionSpec as P


def activate(value):
    return value * jax.nn.sigmoid(value)


def activate_slope(value):
    sigma = jax.nn.sigmoid(value)
    return sigma * (1.0 + value * (1.0 - sigma))


def on_device(states, rates, expert_ids, gate_weights, cotangent, weight_in, weight_out):
    row_count = states.shape[0]
    feature = states.shape[1]
    local_count = weight_in.shape[1]
    groups = lax.axis_size("expert")
    experts_all = local_count * groups
    capacity = max(2, 4 * row_count // experts_all)
    assigned = 2 * row_count
    flat_ids = expert_ids.reshape(assigned)
    onehot = (flat_ids[:, None] == jnp.arange(experts_all, dtype=jnp.int32)[None, :]).astype(
        jnp.int32
    )
    before = jnp.cumsum(onehot, axis=0) - onehot
    slot_index = jnp.sum(before * onehot, axis=1)
    position = flat_ids * capacity + slot_index
    source = jnp.full((experts_all * capacity,), assigned, jnp.int32)
    source = source.at[position].set(jnp.arange(assigned, dtype=jnp.int32))
    zero_row = jnp.zeros((1, feature), jnp.bfloat16)
    padded_states = jnp.concatenate([states, zero_row], axis=0)
    descent = (-gate_weights[:, :, None] * cotangent[:, None, :].astype(jnp.float32)).astype(
        jnp.bfloat16
    )
    padded_descent = jnp.concatenate([descent.reshape(assigned, feature), zero_row], axis=0)
    send_shape = (experts_all, capacity, feature)
    send_knots = padded_states[source // 2].reshape(send_shape)
    send_grads = padded_descent[source].reshape(send_shape)
    got_knots = lax.all_to_all(send_knots, "expert", split_axis=0, concat_axis=0, tiled=True)
    got_grads = lax.all_to_all(send_grads, "expert", split_axis=0, concat_axis=0, tiled=True)
    recv_shape = (groups, local_count, capacity, feature)
    knot_rows = got_knots.reshape(recv_shape)
    grad_rows = got_grads.reshape(recv_shape)
    part = knot_rows
    preact = jnp.einsum(
        "secd,deh->sech",
        part,
        lax.all_gather(weight_in, "fsdp", axis=0, tiled=True),
        preferred_element_type=jnp.float32,
    )
    hidden = activate(preact).astype(jnp.bfloat16)
    part = hidden
    values = jnp.einsum(
        "sech,hed->secd",
        part,
        lax.all_gather(weight_out, "fsdp", axis=0, tiled=True),
        preferred_element_type=jnp.float32,
    )
    slope = jnp.einsum(
        "secd,hed->sech",
        grad_rows,
        lax.all_gather(weight_out, "fsdp", axis=0, tiled=True),
        preferred_element_type=jnp.float32,
    )
    inner = (slope * activate_slope(preact)).astype(jnp.bfloat16)
    returned = jnp.einsum(
        "sech,deh->secd",
        inner,
        lax.all_gather(weight_in, "fsdp", axis=0, tiled=True),
        preferred_element_type=jnp.float32,
    )
    values_send = values.astype(jnp.bfloat16).reshape(send_shape)
    returned_send = returned.astype(jnp.bfloat16).reshape(send_shape)
    values_back = lax.all_to_all(values_send, "expert", split_axis=0, concat_axis=0, tiled=True)
    returned_back = lax.all_to_all(returned_send, "expert", split_axis=0, concat_axis=0, tiled=True)
    values_knot = values_back.reshape(experts_all * capacity, feature)[position]
    values_knot = values_knot.reshape(row_count, 2, feature).astype(jnp.float32)
    combined = jnp.sum(gate_weights[:, :, None] * values_knot, axis=1)
    defect = (rates.astype(jnp.float32) - combined).astype(jnp.bfloat16)
    returned_knot = returned_back.reshape(experts_all * capacity, feature)[position]
    returned_knot = returned_knot.reshape(row_count, 2, feature).astype(jnp.float32)
    grad_states = jnp.sum(returned_knot, axis=1).astype(jnp.bfloat16)
    part = knot_rows
    grad_in = lax.psum_scatter(
        jnp.einsum("secd,sech->deh", part, inner, preferred_element_type=jnp.float32).astype(
            jnp.bfloat16
        ),
        "fsdp",
        scatter_dimension=0,
        tiled=True,
    )
    part = hidden
    grad_out = lax.psum_scatter(
        jnp.einsum("sech,secd->hed", part, grad_rows, preferred_element_type=jnp.float32).astype(
            jnp.bfloat16
        ),
        "fsdp",
        scatter_dimension=0,
        tiled=True,
    )
    return (defect, grad_states, grad_in, grad_out)


def solution(mesh):
    placed = (
        P(("expert", "fsdp"), None),
        P(("expert", "fsdp"), None),
        P(("expert", "fsdp"), None),
        P(("expert", "fsdp"), None),
        P(("expert", "fsdp"), None),
        P("fsdp", "expert", None),
        P("fsdp", "expert", None),
    )
    return jax.shard_map(
        on_device,
        mesh=mesh,
        in_specs=placed,
        out_specs=(
            P(("expert", "fsdp"), None),
            P(("expert", "fsdp"), None),
            P("fsdp", "expert", None),
            P("fsdp", "expert", None),
        ),
        check_vma=False,
    )
```

profile of v0, /device:TPU:1, one launch (start us, length us, event | category | flops | bytes accessed | tf_op | source)
XLA Modules:
  0.0 316.6 jit_solution(13687263189071708302)
XLA Ops:
  7.2 1.6 copy.43
  8.9 1.6 copy.45
  15.8 2.6 gather_fusion
  18.5 16.7 %all-to-all-start = ((bf16[64,8,512]{2,1,0:T(8,128)(2,1)}), bf16[64,8,512]{2,1,0:T(8,128)(2,1)S(1)}, u32[]{:S(2)}, u32[]{:S(2)}) async-start(bf16[64,8,512]{2,1,0:T(8,128)(2,1)} %bitcast.3), calls=%async_computation | async-start | bytes 1048576 | tf_op jit(solution)/shard_map/all_to_all | solution.py:42
  36.2 2.6 gather_fusion.2
  38.8 30.0 %all-to-all-done = bf16[64,8,512]{2,1,0:T(8,128)(2,1)S(1)} async-done(((bf16[64,8,512]{2,1,0:T(8,128)(2,1)}), bf16[64,8,512]{2,1,0:T(8,128)(2,1)S(1)}, u32[]{:S(2)}, u32[]{:S(2)}) %all-to-all-start) | async-done | bytes 524320 | tf_op jit(solution)/shard_map/all_to_all | solution.py:42
  68.8 4.0 %all-to-all-start.2 = ((bf16[64,8,512]{2,1,0:T(8,128)(2,1)}), bf16[64,8,512]{2,1,0:T(8,128)(2,1)S(1)}, u32[]{:S(2)}, u32[]{:S(2)}) async-start(bf16[64,8,512]{2,1,0:T(8,128)(2,1)} %bitcast.13), calls=%async_computation.2 | async-start | bytes 1048576 | tf_op jit(solution)/shard_map/all_to_all | solution.py:43
  72.8 2.8 all-gather.3.cloned.1.call-done
  75.6 3.7 %fusion.12 = (bf16[32,2,8,1024]{3,2,0,1:T(8,128)(2,1)S(1)}, f32[2,32,8,1024]{3,2,1,0:T(8,128)}) fusion(bf16[512,2,1024]{2,0,1:T(8,128)(2,1)} %all-gather.3.cloned.1.call-done, bf16[32,2,8,512]{3,2,1,0:T(8,128)(2,1)S(1)} %bitcast.106), kind=kOutput, calls=%fused_computation.23 | convolution fusion | flops 539492352 | bytes 5767168 | tf_op jit(solution)/shard_map/secd,deh->sech/dot_general | solution.py:48
  79.2 59.6 %all-gather.5.cloned.1.call-done = bf16[1024,2,512]{2,0,1:T(8,128)(2,1)} async-done(((bf16[64,2,512]{2,0,1:T(8,128)(2,1)}), bf16[1024,2,512]{2,0,1:T(8,128)(2,1)}) %all-gather.5.cloned.1.call-update) | async-done | bytes 2097168 | tf_op jit(solution)/shard_map/all_gather | solution.py:59
  138.9 2.3 fusion.28
  142.0 14.6 %all-to-all-start.1 = ((bf16[64,8,512]{2,1,0:T(8,128)(2,1)}), bf16[64,8,512]{2,1,0:T(8,128)(2,1)S(1)}, u32[]{:S(2)}, u32[]{:S(2)}) async-start(bf16[64,8,512]{2,1,0:T(8,128)(2,1)} %bitcast.11), calls=%async_computation.1 | async-start | bytes 1048576 | tf_op jit(solution)/shard_map/all_to_all | solution.py:77
  156.7 2.3 fusion.16
  161.6 2.1 fusion.15
  163.6 6.3 %copy.51 = bf16[512,2,1024]{2,1,0:T(2,128)(2,1)} copy(bf16[512,2,1024]{0,2,1:T(8,128)(2,1)} %fusion.15) | data formatting | bytes 4194304 | tf_op jit(solution)/shard_map/convert_element_type | solution.py:88
  169.9 4.1 %copy.53 = bf16[1024,2,512]{2,1,0:T(2,128)(2,1)} copy(bf16[1024,2,512]{0,2,1:T(8,128)(2,1)S(1)} %fusion.16) | data formatting | bytes 4194304 | tf_op jit(solution)/shard_map/convert_element_type | solution.py:97
  174.0 1.6 copy-done
  175.6 2.0 fusion.25
  178.5 11.6 %all-to-all-done.1 = bf16[64,8,512]{2,1,0:T(8,128)(2,1)S(1)} async-done(((bf16[64,8,512]{2,1,0:T(8,128)(2,1)}), bf16[64,8,512]{2,1,0:T(8,128)(2,1)S(1)}, u32[]{:S(2)}, u32[]{:S(2)}) %all-to-all-start.1) | async-done | bytes 524320 | tf_op jit(solution)/shard_map/all_to_all | solution.py:77
  190.1 4.1 %all-to-all-start.3 = ((bf16[64,8,512]{2,1,0:T(8,128)(2,1)}), bf16[64,8,512]{2,1,0:T(8,128)(2,1)S(1)}, u32[]{:S(2)}, u32[]{:S(2)}) async-start(bf16[64,8,512]{2,1,0:T(8,128)(2,1)} %bitcast.19), calls=%async_computation.3 | async-start | bytes 1048576 | tf_op jit(solution)/shard_map/all_to_all | solution.py:78
  198.0 29.7 %all-to-all-done.3 = bf16[64,8,512]{2,1,0:T(8,128)(2,1)S(1)} async-done(((bf16[64,8,512]{2,1,0:T(8,128)(2,1)}), bf16[64,8,512]{2,1,0:T(8,128)(2,1)S(1)}, u32[]{:S(2)}, u32[]{:S(2)}) %all-to-all-start.3) | async-done | bytes 524320 | tf_op jit(solution)/shard_map/all_to_all | solution.py:78
  232.0 74.8 %all-reduce.7.cloned.1.call-done = (bf16[512,2,1024]{2,1,0:T(2,128)(2,1)}, bf16[1024,2,512]{2,1,0:T(2,128)(2,1)}) async-done(((bf16[512,2,1024]{2,1,0:T(2,128)(2,1)}, bf16[1024,2,512]{2,1,0:T(2,128)(2,1)}), (bf16[512,2,1024]{2,1,0:T(2,128)(2,1)}, bf16[1024,2,512]{2,1,0:T(2,128)(2,1)})) %all-reduce.7.cloned.1.call-update) | async-done | bytes 4194320
  306.8 1.6 constant_dynamic-slice_fusion.1
  308.4 1.6 constant_dynamic-slice_fusion
  (64 shorter events, 17.5 us)
Async XLA Ops:
  7.2 68.4 %all-gather.3.cloned.1.call-start = ((), (), s32[]{:S(2)}) async-start(), calls=%async_computation.4 | async-start | bytes 2228224 | tf_op jit(solution)/shard_map/all_gather | solution.py:51
  8.8 130.1 %all-gather.5.cloned.1.call-start = ((), (), s32[]{:S(2)}) async-start(), calls=%async_computation.5 | async-start | bytes 2228224 | tf_op jit(solution)/shard_map/all_gather | solution.py:59
  15.8 19.4 %copy-start.8 = (f32[128,2]{0,1:T(2,128)S(1)}, f32[128,2]{0,1:T(2,128)}, u32[]{:S(2)}) copy-start(f32[128,2]{0,1:T(2,128)} %param.10) | copy-start | bytes 3076
  15.8 19.7 %copy-start.6 = (bf16[128,512]{1,0:T(8,128)(2,1)S(1)}, bf16[128,512]{1,0:T(8,128)(2,1)}, u32[]{:S(2)}) copy-start(bf16[128,512]{1,0:T(8,128)(2,1)} %param.11) | copy-start | bytes 393220
  18.5 50.3 %all-to-all-start = ((bf16[64,8,512]{2,1,0:T(8,128)(2,1)}), bf16[64,8,512]{2,1,0:T(8,128)(2,1)S(1)}, u32[]{:S(2)}, u32[]{:S(2)}) async-start(bf16[64,8,512]{2,1,0:T(8,128)(2,1)} %bitcast.3), calls=%async_computation | async-start | bytes 1048576 | tf_op jit(solution)/shard_map/all_to_all | solution.py:42
  68.8 73.3 %all-to-all-start.2 = ((bf16[64,8,512]{2,1,0:T(8,128)(2,1)}), bf16[64,8,512]{2,1,0:T(8,128)(2,1)S(1)}, u32[]{:S(2)}, u32[]{:S(2)}) async-start(bf16[64,8,512]{2,1,0:T(8,128)(2,1)} %bitcast.13), calls=%async_computation.2 | async-start | bytes 1048576 | tf_op jit(solution)/shard_map/all_to_all | solution.py:43
  79.2 62.8 %copy-start.2 = (bf16[32,2,8,1024]{3,2,0,1:T(8,128)(2,1)}, bf16[32,2,8,1024]{3,2,0,1:T(8,128)(2,1)S(1)}, u32[]{:S(2)}) copy-start(bf16[32,2,8,1024]{3,2,0,1:T(8,128)(2,1)S(1)} %get-tuple-element.16) | copy-start | bytes 3145732
  142.0 14.6 %copy-start.4 = (bf16[64,8,512]{2,1,0:T(8,128)(2,1)}, bf16[64,8,512]{2,1,0:T(8,128)(2,1)S(1)}, u32[]{:S(2)}) copy-start(bf16[64,8,512]{2,1,0:T(8,128)(2,1)S(1)} %all-to-all-done.2) | copy-start | bytes 1572868
  142.0 48.1 %all-to-all-start.1 = ((bf16[64,8,512]{2,1,0:T(8,128)(2,1)}), bf16[64,8,512]{2,1,0:T(8,128)(2,1)S(1)}, u32[]{:S(2)}, u32[]{:S(2)}) async-start(bf16[64,8,512]{2,1,0:T(8,128)(2,1)} %bitcast.11), calls=%async_computation.1 | async-start | bytes 1048576 | tf_op jit(solution)/shard_map/all_to_all | solution.py:77
  156.6 150.2 %all-reduce.7.cloned.1.call-start = ((), (), s32[]{:S(2)}) async-start(), calls=%async_computation.6 | async-start | bytes 8388608
  156.7 2.3 copy-start.1
  156.7 2.3 copy-start.5
  156.7 2.8 copy-start.9
  160.6 1.0 copy-start.3
  174.0 1.6 copy-start
  190.1 37.6 %all-to-all-start.3 = ((bf16[64,8,512]{2,1,0:T(8,128)(2,1)}), bf16[64,8,512]{2,1,0:T(8,128)(2,1)S(1)}, u32[]{:S(2)}, u32[]{:S(2)}) async-start(bf16[64,8,512]{2,1,0:T(8,128)(2,1)} %bitcast.19), calls=%async_computation.3 | async-start | bytes 1048576 | tf_op jit(solution)/shard_map/all_to_all | solution.py:78
  227.7 3.6 %copy-start.7 = (bf16[128,512]{1,0:T(8,128)(2,1)S(1)}, bf16[128,512]{1,0:T(8,128)(2,1)}, u32[]{:S(2)}) copy-start(bf16[128,512]{1,0:T(8,128)(2,1)} %param.8) | copy-start | bytes 393220
Sparse Core Ops, SparseCore 0:
  11.6 63.9 all-gather.2
  79.2 59.6 all-gather.4
  174.2 132.5 all-reduce.6
where the time goes:
time: 318 us; the launch traced here: 317 us
  waiting for transfers between devices  208 us (65%)
  starting transfers between devices  39.5 us (12%)
  local copies, waits for them, and re-layouts  35.6 us (11%)
  between operations  15.3 us (5%)
  matrix products  13.3 us (4%)
  other arithmetic  4.29 us (1%)
    unnamed x4, waiting for transfers between devices  74.8 us
    all_gather x1, waiting for transfers between devices, on_device(): lax.all_gather(weight_out, 'fsdp', axis=0, tiled=True)  59.6 us
    all_to_all x1, waiting for transfers between devices, on_device(): lax.all_to_all(send_knots, 'expert', split_axis=0, concat_axis=0, tiled=T...  30 us
    all_to_all x1, waiting for transfers between devices, on_device(): lax.all_to_all(returned_send, 'expert', split_axis=0, concat_axis=0, tile...  29.7 us
    all_to_all x1, starting transfers between devices, on_device(): lax.all_to_all(send_knots, 'expert', split_axis=0, concat_axis=0, tiled=T...  16.7 us
    all_to_all x1, starting transfers between devices, on_device(): lax.all_to_all(values_send, 'expert', split_axis=0, concat_axis=0, tiled=...  14.6 us
    unnamed x27, local copies, waits for them, and re-layouts  11.7 us
    all_to_all x1, waiting for transfers between devices, on_device(): lax.all_to_all(values_send, 'expert', split_axis=0, concat_axis=0, tiled=...  11.6 us
  transfers between devices with their start and end apart: 7, of which 6 were waited for; matrix products, arithmetic and copies ran while one was open for 14% of the time, Pallas kernels for 0%

commit v1 on v0

v1 whole, which is shorter than its diff:
```python
import jax
import jax.numpy as jnp
from jax import lax
from jax.sharding import PartitionSpec as P


def activate(value):
    return value * jax.nn.sigmoid(value)


def activate_slope(value):
    sigma = jax.nn.sigmoid(value)
    return sigma * (1.0 + value * (1.0 - sigma))


def grid_of(count):
    cols = 1
    for c in range(1, count + 1):
        if count % c == 0 and c * c <= count:
            cols = c
    return count // cols, cols


def shift_pairs(count, rows, cols, step, along_cols):
    pairs = []
    for f in range(count):
        r, c = divmod(f, cols)
        if along_cols:
            g = r * cols + (c + step) % cols
        else:
            g = ((r + step) % rows) * cols + c
        pairs.append((f, g))
    return pairs


def ring_gather(piece, rows, cols):
    count = rows * cols
    f = lax.axis_index("fsdp")
    r, c = f // cols, f % cols
    got = [piece] + [
        lax.ppermute(piece, "fsdp", shift_pairs(count, rows, cols, s, True)) for s in range(1, cols)
    ]
    rev = jnp.stack([got[(-k) % cols] for k in range(cols)])
    row = jnp.roll(rev, c, axis=0)
    got = [row] + [
        lax.ppermute(row, "fsdp", shift_pairs(count, rows, cols, s, False)) for s in range(1, rows)
    ]
    rev = jnp.stack([got[(-k) % rows] for k in range(rows)])
    whole = jnp.roll(rev, r, axis=0)
    return whole.reshape(count, piece.shape[0])


def ring_reduce_scatter(chunks, rows, cols):
    count = rows * cols
    f = lax.axis_index("fsdp")
    r, c = f // cols, f % cols
    grid = chunks.reshape(rows, cols, chunks.shape[1])
    total = lax.dynamic_index_in_dim(grid, r, 0, keepdims=False).astype(jnp.float32)
    for s in range(1, rows):
        part = lax.dynamic_index_in_dim(grid, (r + s) % rows, 0, keepdims=False)
        total = total + lax.ppermute(part, "fsdp", shift_pairs(count, rows, cols, s, False)).astype(
            jnp.float32
        )
    mine = lax.dynamic_index_in_dim(total, c, 0, keepdims=False)
    for s in range(1, cols):
        part = lax.dynamic_index_in_dim(total, (c + s) % cols, 0, keepdims=False)
        mine = mine + lax.ppermute(part, "fsdp", shift_pairs(count, rows, cols, s, True))
    return mine


def on_device(states, rates, expert_ids, gate_weights, cotangent, weight_in, weight_out):
    row_count = states.shape[0]
    feature = states.shape[1]
    local_count = weight_in.shape[1]
    hidden_width = weight_in.shape[2]
    groups = lax.axis_size("expert")
    fsdp_count = lax.axis_size("fsdp")
    rows, cols = grid_of(fsdp_count)
    experts_all = local_count * groups
    capacity = max(2, 4 * row_count // experts_all)
    assigned = 2 * row_count

    in_size = weight_in.size
    pieces = jnp.concatenate([weight_in.reshape(-1), weight_out.reshape(-1)])
    gathered = ring_gather(pieces, rows, cols)
    full_in = gathered[:, :in_size].reshape((fsdp_count * weight_in.shape[0],) + weight_in.shape[1:])
    full_out = gathered[:, in_size:].reshape((fsdp_count * weight_out.shape[0],) + weight_out.shape[1:])

    flat_ids = expert_ids.reshape(assigned)
    onehot = (flat_ids[:, None] == jnp.arange(experts_all, dtype=jnp.int32)[None, :]).astype(
        jnp.int32
    )
    before = jnp.cumsum(onehot, axis=0) - onehot
    slot_index = jnp.sum(before * onehot, axis=1)
    position = flat_ids * capacity + slot_index
    source = jnp.full((experts_all * capacity,), assigned, jnp.int32)
    source = source.at[position].set(jnp.arange(assigned, dtype=jnp.int32))
    zero_row = jnp.zeros((1, feature), jnp.bfloat16)
    padded_states = jnp.concatenate([states, zero_row], axis=0)
    descent = (-gate_weights[:, :, None] * cotangent[:, None, :].astype(jnp.float32)).astype(
        jnp.bfloat16
    )
    padded_descent = jnp.concatenate([descent.reshape(assigned, feature), zero_row], axis=0)
    send_shape = (experts_all, capacity, feature)
    send_knots = padded_states[source // 2].reshape(send_shape)
    send_grads = padded_descent[source].reshape(send_shape)
    send = jnp.concatenate([send_knots, send_grads], axis=1)
    got = lax.all_to_all(send, "expert", split_axis=0, concat_axis=0, tiled=True)
    got = got.reshape(groups, local_count, 2 * capacity, feature)
    knot_rows = got[:, :, :capacity]
    grad_rows = got[:, :, capacity:]

    preact = jnp.einsum("secd,deh->sech", knot_rows, full_in, preferred_element_type=jnp.float32)
    hidden = activate(preact).astype(jnp.bfloat16)
    values = jnp.einsum("sech,hed->secd", hidden, full_out, preferred_element_type=jnp.float32)
    slope = jnp.einsum("secd,hed->sech", grad_rows, full_out, preferred_element_type=jnp.float32)
    inner = (slope * activate_slope(preact)).astype(jnp.bfloat16)

    part_in = jnp.einsum(
        "secd,sech->deh", knot_rows, inner, preferred_element_type=jnp.float32
    ).astype(jnp.bfloat16)
    part_out = jnp.einsum(
        "sech,secd->hed", hidden, grad_rows, preferred_element_type=jnp.float32
    ).astype(jnp.bfloat16)
    chunks = jnp.concatenate(
        [part_in.reshape(fsdp_count, -1), part_out.reshape(fsdp_count, -1)], axis=1
    )
    summed = ring_reduce_scatter(chunks, rows, cols).astype(jnp.bfloat16)
    grad_in = summed[:in_size].reshape(weight_in.shape)
    grad_out = summed[in_size:].reshape(weight_out.shape)

    returned = jnp.einsum("sech,deh->secd", inner, full_in, preferred_element_type=jnp.float32)
    back = jnp.concatenate(
        [values.astype(jnp.bfloat16), returned.astype(jnp.bfloat16)], axis=2
    ).reshape(experts_all, 2 * capacity, feature)
    back = lax.all_to_all(back, "expert", split_axis=0, concat_axis=0, tiled=True)
    back = back.reshape(experts_all * capacity * 2, feature)
    values_knot = back[(position // capacity) * (2 * capacity) + position % capacity]
    values_knot = values_knot.reshape(row_count, 2, feature).astype(jnp.float32)
    combined = jnp.sum(gate_weights[:, :, None] * values_knot, axis=1)
    defect = (rates.astype(jnp.float32) - combined).astype(jnp.bfloat16)
    returned_knot = back[(position // capacity) * (2 * capacity) + capacity + position % capacity]
    returned_knot = returned_knot.reshape(row_count, 2, feature).astype(jnp.float32)
    grad_states = jnp.sum(returned_knot, axis=1).astype(jnp.bfloat16)
    return (defect, grad_states, grad_in, grad_out)


def solution(mesh):
    placed = (
        P(("expert", "fsdp"), None),
        P(("expert", "fsdp"), None),
        P(("expert", "fsdp"), None),
        P(("expert", "fsdp"), None),
        P(("expert", "fsdp"), None),
        P("fsdp", "expert", None),
        P("fsdp", "expert", None),
    )
    return jax.shard_map(
        on_device,
        mesh=mesh,
        in_specs=placed,
        out_specs=(
            P(("expert", "fsdp"), None),
            P(("expert", "fsdp"), None),
            P("fsdp", "expert", None),
            P("fsdp", "expert", None),
        ),
        check_vma=False,
    )
```

time: 318 us -> 327 us (1.028)
  waiting for transfers between devices: 208 us -> 144 us
  local copies, waits for them, and re-layouts: 35.6 us -> 92.6 us
  starting transfers between devices: 39.5 us -> 70.4 us
  between operations: 15.3 us -> 1.45 us
  matrix products: 13.3 us -> 8.85 us
  other arithmetic: 4.29 us -> 8.22 us
    ppermute x0 -> x12, waiting for transfers between devices: none -> 92.9 us  [the longest x3 43.6 us: ring_reduce_scatter(): lax.ppermute(part, 'fsdp', shift_pairs(count, rows, cols, s, False))]
    unnamed x4 -> x0, waiting for transfers between devices: 74.8 us -> none
    all_gather x2 -> x0, waiting for transfers between devices: 62.4 us -> none  [the longest x1 59.6 us: on_device(): lax.all_gather(weight_out, 'fsdp', axis=0, tiled=True)]
    ppermute x0 -> x12, starting transfers between devices: none -> 40.2 us  [the longest x3 13.5 us: ring_gather(): lax.ppermute(row, 'fsdp', shift_pairs(count, rows, cols, s, False))]
    concatenate x0 -> x7, local copies, waits for them, and re-layouts: none -> 21.2 us  [the longest x1 10.3 us: ring_gather(): row = jnp.roll(rev, c, axis=0)]
    all_to_all x4 -> x2, waiting for transfers between devices: 71.3 us -> 50.9 us  [the longest x1 50.9 us: on_device(): lax.all_to_all(back, 'expert', split_axis=0, concat_axis=0, tiled=True)]
    reshape x0 -> x3, local copies, waits for them, and re-layouts: none -> 10.9 us  [the longest x1 4.06 us: ring_gather(): return whole.reshape(count, piece.shape[0])]
    all_to_all x4 -> x2, starting transfers between devices: 39.4 us -> 30.1 us  [the longest x1 16.1 us: on_device(): lax.all_to_all(send, 'expert', split_axis=0, concat_axis=0, tiled=True)]
  transfers between devices with their start and end apart: 7 -> 14, of which waited for: 6 -> 8; matrix products, arithmetic and copies ran while one was open for 14% -> 15% of each run, Pallas kernels for 0% -> 0%
where the time goes in v1:
time: 327 us; the launch traced here: 325 us
  waiting for transfers between devices  144 us (44%)
  local copies, waits for them, and re-layouts  92.6 us (28%)
  starting transfers between devices  70.4 us (22%)
  matrix products  8.85 us (3%)
  other arithmetic  8.22 us (3%)
    all_to_all x1, waiting for transfers between devices, on_device(): lax.all_to_all(back, 'expert', split_axis=0, concat_axis=0, tiled=True)  50.9 us
    ppermute x3, waiting for transfers between devices, ring_reduce_scatter(): lax.ppermute(part, 'fsdp', shift_pairs(count, rows, cols, s, False))  43.6 us
    ppermute x3, waiting for transfers between devices, ring_gather(): lax.ppermute(row, 'fsdp', shift_pairs(count, rows, cols, s, False))  43.2 us
    unnamed x45, local copies, waits for them, and re-layouts  18.2 us
    all_to_all x1, starting transfers between devices, on_device(): lax.all_to_all(send, 'expert', split_axis=0, concat_axis=0, tiled=True)  16.1 us
    all_to_all x1, starting transfers between devices, on_device(): lax.all_to_all(back, 'expert', split_axis=0, concat_axis=0, tiled=True)  14.1 us
    ppermute x3, starting transfers between devices, ring_gather(): lax.ppermute(row, 'fsdp', shift_pairs(count, rows, cols, s, False))  13.5 us
    concatenate x1, local copies, waits for them, and re-layouts, ring_gather(): row = jnp.roll(rev, c, axis=0)  10.3 us
  transfers between devices with their start and end apart: 14, of which 8 were waited for; matrix products, arithmetic and copies ran while one was open for 15% of the time, Pallas kernels for 0%

profile of v1, /device:TPU:1, one launch (start us, length us, event | category | flops | bytes accessed | tf_op | source)
XLA Modules:
  0.0 325.3 jit_solution(11569284673853021925)
XLA Ops:
  2.6 5.2 %collective-permute-start = (bf16[131072]{0:T(1024)(128)(2,1)S(1)}, bf16[131072]{0:T(1024)(128)(2,1)S(1)}, u32[]{:S(2)}, u32[]{:S(2)}) collective-permute-start(bf16[131072]{0:T(1024)(128)(2,1)S(1)} %constant_dynamic-update-slice_fusion.3), channel_id=1, source_target_pairs={{0,3},{1,0},{2,1},{3,2},{4,7},{5,4},{6,5},{7,6},{8,11},{9,8},{10,9... | collective-permute-start | bytes 786440 | tf_op jit(solution)/shard_map/ppermute | solution.py:41
  18.3 2.9 collective-permute-done.2
  22.3 10.3 %concatenate.34 = bf16[8,131072]{1,0:T(8,128)(2,1)S(1)} concatenate(bf16[1,131072]{1,0:T(2,128)(2,1)S(1)} %stack.26, bf16[1,131072]{1,0:T(2,128)(2,1)S(1)} %stack.27, bf16[1,131072]{1,0:T(2,128)(2,1)} %stack.28, bf16[1,131072]{1,0:T(2,128)(2,1)} %stack.29, bf16[1,131072]{1,0:T(2,128)(2,1)S(1)} %stack.26, bf16[1,131072]{1,0:T(2,128)(2,1)S(1)} %stack.27, bf16[1,131072]{1,0:T(2,128)(2,1)} %stack.28, ...), dimensions={0} | concatenate | bytes 4194304 | tf_op jit(solution)/shard_map/jit(_roll_dynamic)/concatenate | solution.py:44
  34.2 8.5 %collective-permute-start.3 = (bf16[4,131072]{1,0:T(4,128)(2,1)S(1)}, bf16[4,131072]{1,0:T(4,128)(2,1)S(1)}, u32[]{:S(2)}, u32[]{:S(2)}) collective-permute-start(bf16[4,131072]{1,0:T(4,128)(2,1)S(1)} %get-tuple-element.8), channel_id=1, source_target_pairs={{0,12},{1,13},{2,14},{3,15},{4,0},{5,1},{6,2},{7,3},{8,4},{9,5},{1... | collective-permute-start | bytes 3145736 | tf_op jit(solution)/shard_map/ppermute | solution.py:46
  51.4 16.1 %all-to-all-start = ((bf16[64,16,512]{2,1,0:T(8,128)(2,1)}), bf16[64,16,512]{2,1,0:T(8,128)(2,1)}, u32[]{:S(2)}, u32[]{:S(2)}) async-start(bf16[64,16,512]{2,1,0:T(8,128)(2,1)} %pad_maximum_fusion), calls=%async_computation | async-start | bytes 2097152 | tf_op jit(solution)/shard_map/all_to_all | solution.py:108
  69.8 2.8 collective-permute-start.5
  73.9 21.6 %collective-permute-done.4 = bf16[4,131072]{1,0:T(4,128)(2,1)S(1)} collective-permute-done((bf16[4,131072]{1,0:T(4,128)(2,1)S(1)}, bf16[4,131072]{1,0:T(4,128)(2,1)S(1)}, u32[]{:S(2)}, u32[]{:S(2)}) %collective-permute-start.4) | collective-permute-done | bytes 1048608 | tf_op jit(solution)/shard_map/ppermute | solution.py:46
  96.8 21.6 %collective-permute-done.5 = bf16[4,131072]{1,0:T(4,128)(2,1)S(1)} collective-permute-done((bf16[4,131072]{1,0:T(4,128)(2,1)S(1)}, bf16[4,131072]{1,0:T(4,128)(2,1)S(1)}, u32[]{:S(2)}, u32[]{:S(2)}) %collective-permute-start.5) | collective-permute-done | bytes 1048608 | tf_op jit(solution)/shard_map/ppermute | solution.py:46
  125.3 5.6 %constant_dynamic-slice_fusion.4 = bf16[4,4,131072]{2,1,0:T(4,128)(2,1)} fusion(bf16[8,4,131072]{2,1,0:T(4,128)(2,1)} %bitcast_dynamic-update-slice_fusion.1, s32[]{:T(128)S(6)} %select_n.168), kind=kLoop, calls=%fused_computation.87 | loop fusion | bytes 8388612 | tf_op jit(solution)/shard_map/jit(_roll_dynamic)/dynamic_slice | solution.py:49
  130.9 4.1 %reshape.235 = bf16[16,131072]{1,0:T(8,128)(2,1)} reshape(bf16[4,4,131072]{2,1,0:T(4,128)(2,1)} %constant_dynamic-slice_fusion.4) | data formatting | bytes 8388608 | tf_op jit(solution)/shard_map/reshape | solution.py:50
  135.0 3.9 %fusion.49 = (bf16[16,65536]{1,0:T(8,128)(2,1)S(1)}, bf16[16,65536]{1,0:T(8,128)(2,1)}) fusion(bf16[16,131072]{1,0:T(8,128)(2,1)} %reshape.235), kind=kLoop, calls=%fused_computation.100 | loop fusion | bytes 8388608 | tf_op jit(solution)/shard_map/slice | solution.py:87
  138.8 4.0 %reshape.237 = bf16[512,2,1024]{2,1,0:T(2,128)(2,1)} reshape(bf16[16,65536]{1,0:T(8,128)(2,1)} %get-tuple-element.13) | data formatting | bytes 4194304 | tf_op jit(solution)/shard_map/reshape | solution.py:86
  142.8 2.8 reshape.236
  156.3 5.0 %copy.25 = bf16[512,2,1024]{2,1,0:T(2,128)(2,1)S(1)} copy(bf16[512,2,1024]{0,2,1:T(8,128)(2,1)} %fusion.17) | data formatting | bytes 4194304 | tf_op jit(solution)/shard_map/convert_element_type | solution.py:121
  164.0 3.8 %constant_dynamic-update-slice_fusion.2 = bf16[4,4,131072]{2,1,0:T(4,128)(2,1)} fusion(bf16[4,4,65536]{2,1,0:T(4,128)(2,1)} %concatenate.40), kind=kLoop, calls=%fused_computation.67 | loop fusion | bytes 4194304
  167.8 4.0 %copy.26 = bf16[1024,2,512]{2,1,0:T(2,128)(2,1)} copy(bf16[1024,2,512]{0,2,1:T(8,128)(2,1)S(1)} %copy-done.4) | data formatting | bytes 4194304 | tf_op jit(solution)/shard_map/convert_element_type | solution.py:124
  171.8 3.2 concatenate.41
  177.0 4.3 %dynamic-slice_bitcast_fusion.2 = (bf16[4,131072]{1,0:T(4,128)(2,1)}, bf16[4,131072]{1,0:T(4,128)(2,1)}, bf16[4,131072]{1,0:T(4,128)(2,1)}) fusion(bf16[4,4,131072]{2,1,0:T(4,128)(2,1)} %constant_dynamic-update-slice_fusion.1, s32[]{:T(128)S(6)} %select_n.179, s32[]{:T(128)S(6)} %select_n.183, s32[]{:T(128)S(6)} %select_n.181), kind=kLoop, calls=%fused_computation.47 | loop fusion | bytes 6291468 | tf_op jit(solution)/shard_map/jit(dynamic_index_in_dim)/squeeze | solution.py:60
  186.0 4.0 %collective-permute-start.8 = (bf16[4,131072]{1,0:T(4,128)(2,1)}, bf16[4,131072]{1,0:T(4,128)(2,1)S(1)}, u32[]{:S(2)}, u32[]{:S(2)}) collective-permute-start(bf16[4,131072]{1,0:T(4,128)(2,1)} %get-tuple-element.10), channel_id=1, source_target_pairs={{0,12},{1,13},{2,14},{3,15},{4,0},{5,1},{6,2},{7,3},{8,4},{9,5},{1... | collective-permute-start | bytes 3145736 | tf_op jit(solution)/shard_map/ppermute | solution.py:61
  190.2 41.1 %collective-permute-done.6 = bf16[4,131072]{1,0:T(4,128)(2,1)S(1)} collective-permute-done((bf16[4,131072]{1,0:T(4,128)(2,1)}, bf16[4,131072]{1,0:T(4,128)(2,1)S(1)}, u32[]{:S(2)}, u32[]{:S(2)}) %collective-permute-start.6) | collective-permute-done | bytes 1048608 | tf_op jit(solution)/shard_map/ppermute | solution.py:61
  241.2 2.8 collective-permute-start.11
  250.1 14.1 %all-to-all-start.1 = ((bf16[64,16,512]{2,1,0:T(8,128)(2,1)}), bf16[64,16,512]{2,1,0:T(8,128)(2,1)S(1)}, u32[]{:S(2)}, u32[]{:S(2)}) async-start(bf16[64,16,512]{2,1,0:T(8,128)(2,1)} %bitcast.18), calls=%async_computation.1 | async-start | bytes 2097152 | tf_op jit(solution)/shard_map/all_to_all | solution.py:136
  264.4 3.0 collective-permute-done.9
  268.9 50.9 %all-to-all-done.1 = bf16[64,16,512]{2,1,0:T(8,128)(2,1)S(1)} async-done(((bf16[64,16,512]{2,1,0:T(8,128)(2,1)}), bf16[64,16,512]{2,1,0:T(8,128)(2,1)S(1)}, u32[]{:S(2)}, u32[]{:S(2)}) %all-to-all-start.1) | async-done | bytes 1048608 | tf_op jit(solution)/shard_map/all_to_all | solution.py:136
  (119 shorter events, 78.4 us)
Async XLA Ops:
  0.6 14.4 %copy-start.10 = (s32[128,2]{0,1:T(2,128)S(1)}, s32[128,2]{0,1:T(2,128)}, u32[]{:S(2)}) copy-start(s32[128,2]{0,1:T(2,128)} %param.9) | copy-start | bytes 3076
  0.6 14.6 %copy-start.6 = (bf16[128,512]{1,0:T(8,128)(2,1)S(1)}, bf16[128,512]{1,0:T(8,128)(2,1)}, u32[]{:S(2)}) copy-start(bf16[128,512]{1,0:T(8,128)(2,1)} %param.11) | copy-start | bytes 393220
  0.7 16.0 %copy-start.11 = (f32[128,2]{0,1:T(2,128)S(1)}, f32[128,2]{0,1:T(2,128)}, u32[]{:S(2)}) copy-start(f32[128,2]{0,1:T(2,128)} %param.10) | copy-start | bytes 3076
  2.6 14.3 %collective-permute-start = (bf16[131072]{0:T(1024)(128)(2,1)S(1)}, bf16[131072]{0:T(1024)(128)(2,1)S(1)}, u32[]{:S(2)}, u32[]{:S(2)}) collective-permute-start(bf16[131072]{0:T(1024)(128)(2,1)S(1)} %constant_dynamic-update-slice_fusion.3), channel_id=1, source_target_pairs={{0,3},{1,0},{2,1},{3,2},{4,7},{5,4},{6,5},{7,6},{8,11},{9,8},{10,9... | collective-permute-start | bytes 786440 | tf_op jit(solution)/shard_map/ppermute | solution.py:41
  7.8 9.4 %collective-permute-start.1 = (bf16[131072]{0:T(1024)(128)(2,1)S(1)}, bf16[131072]{0:T(1024)(128)(2,1)S(1)}, u32[]{:S(2)}, u32[]{:S(2)}) collective-permute-start(bf16[131072]{0:T(1024)(128)(2,1)S(1)} %constant_dynamic-update-slice_fusion.3), channel_id=1, source_target_pairs={{0,2},{1,3},{2,0},{3,1},{4,6},{5,7},{6,4},{7,5},{8,10},{9,11},{10,... | collective-permute-start | bytes 786440 | tf_op jit(solution)/shard_map/ppermute | solution.py:41
  10.3 11.0 %collective-permute-start.2 = (bf16[131072]{0:T(1024)(128)(2,1)S(1)}, bf16[131072]{0:T(1024)(128)(2,1)S(1)}, u32[]{:S(2)}, u32[]{:S(2)}) collective-permute-start(bf16[131072]{0:T(1024)(128)(2,1)S(1)} %constant_dynamic-update-slice_fusion.3), channel_id=1, source_target_pairs={{0,1},{1,2},{2,3},{3,0},{4,5},{5,6},{6,7},{7,4},{8,9},{9,10},{10,1... | collective-permute-start | bytes 786440 | tf_op jit(solution)/shard_map/ppermute | solution.py:41
  15.0 7.3 %copy-start.9 = (s32[64,3]{0,1:T(4,128)}, s32[64,3]{0,1:T(4,128)S(1)}, u32[]{:S(2)}) copy-start(s32[64,3]{0,1:T(4,128)S(1)} %reduce-window.9) | copy-start | bytes 2308
  32.7 10.1 %copy-start.5 = (f32[256,512]{1,0:T(8,128)S(1)}, f32[256,512]{1,0:T(8,128)}, u32[]{:S(2)}) copy-start(f32[256,512]{1,0:T(8,128)} %mul.84) | copy-start | bytes 1572868
  32.7 10.2 %copy-start.7 = (bf16[128,512]{1,0:T(8,128)(2,1)S(1)}, bf16[128,512]{1,0:T(8,128)(2,1)}, u32[]{:S(2)}) copy-start(bf16[128,512]{1,0:T(8,128)(2,1)} %param.7) | copy-start | bytes 393220
  32.7 10.2 %slice-start = ((s32[64,3]{0,1:T(4,128)}), s32[64,2]{0,1:T(2,128)S(1)}, s32[]{:S(2)}) async-start(s32[64,3]{0,1:T(4,128)} %copy-done.9), calls=%async_computation.2 | async-start | bytes 2048 | tf_op jit(solution)/shard_map/slice.1
  34.2 38.4 %collective-permute-start.3 = (bf16[4,131072]{1,0:T(4,128)(2,1)S(1)}, bf16[4,131072]{1,0:T(4,128)(2,1)S(1)}, u32[]{:S(2)}, u32[]{:S(2)}) collective-permute-start(bf16[4,131072]{1,0:T(4,128)(2,1)S(1)} %get-tuple-element.8), channel_id=1, source_target_pairs={{0,12},{1,13},{2,14},{3,15},{4,0},{5,1},{6,2},{7,3},{8,4},{9,5},{1... | collective-permute-start | bytes 3145736 | tf_op jit(solution)/shard_map/ppermute | solution.py:46
  51.4 94.3 %all-to-all-start = ((bf16[64,16,512]{2,1,0:T(8,128)(2,1)}), bf16[64,16,512]{2,1,0:T(8,128)(2,1)}, u32[]{:S(2)}, u32[]{:S(2)}) async-start(bf16[64,16,512]{2,1,0:T(8,128)(2,1)} %pad_maximum_fusion), calls=%async_computation | async-start | bytes 2097152 | tf_op jit(solution)/shard_map/all_to_all | solution.py:108
  67.5 28.0 %collective-permute-start.4 = (bf16[4,131072]{1,0:T(4,128)(2,1)S(1)}, bf16[4,131072]{1,0:T(4,128)(2,1)S(1)}, u32[]{:S(2)}, u32[]{:S(2)}) collective-permute-start(bf16[4,131072]{1,0:T(4,128)(2,1)S(1)} %get-tuple-element.8), channel_id=1, source_target_pairs={{0,8},{1,9},{2,10},{3,11},{4,12},{5,13},{6,14},{7,15},{8,0},{9,1},... | collective-permute-start | bytes 3145736 | tf_op jit(solution)/shard_map/ppermute | solution.py:46
  69.8 48.7 %collective-permute-start.5 = (bf16[4,131072]{1,0:T(4,128)(2,1)S(1)}, bf16[4,131072]{1,0:T(4,128)(2,1)S(1)}, u32[]{:S(2)}, u32[]{:S(2)}) collective-permute-start(bf16[4,131072]{1,0:T(4,128)(2,1)S(1)} %get-tuple-element.8), channel_id=1, source_target_pairs={{0,4},{1,5},{2,6},{3,7},{4,8},{5,9},{6,10},{7,11},{8,12},{9,13},{1... | collective-permute-start | bytes 3145736 | tf_op jit(solution)/shard_map/ppermute | solution.py:46
  164.0 3.8 %copy-start.4 = (bf16[1024,2,512]{0,2,1:T(8,128)(2,1)S(1)}, bf16[1024,2,512]{0,2,1:T(8,128)(2,1)}, u32[]{:S(2)}) copy-start(bf16[1024,2,512]{0,2,1:T(8,128)(2,1)} %fusion.18) | copy-start | bytes 6291460
  181.3 50.0 %collective-permute-start.6 = (bf16[4,131072]{1,0:T(4,128)(2,1)}, bf16[4,131072]{1,0:T(4,128)(2,1)S(1)}, u32[]{:S(2)}, u32[]{:S(2)}) collective-permute-start(bf16[4,131072]{1,0:T(4,128)(2,1)} %get-tuple-element.9), channel_id=1, source_target_pairs={{0,4},{1,5},{2,6},{3,7},{4,8},{5,9},{6,10},{7,11},{8,12},{9,13},{1... | collective-permute-start | bytes 3145736 | tf_op jit(solution)/shard_map/ppermute | solution.py:61
  183.2 48.1 %collective-permute-start.7 = (bf16[4,131072]{1,0:T(4,128)(2,1)}, bf16[4,131072]{1,0:T(4,128)(2,1)S(1)}, u32[]{:S(2)}, u32[]{:S(2)}) collective-permute-start(bf16[4,131072]{1,0:T(4,128)(2,1)} %get-tuple-element.11), channel_id=1, source_target_pairs={{0,8},{1,9},{2,10},{3,11},{4,12},{5,13},{6,14},{7,15},{8,0},{9,1},... | collective-permute-start | bytes 3145736 | tf_op jit(solution)/shard_map/ppermute | solution.py:61
  186.0 47.8 %collective-permute-start.8 = (bf16[4,131072]{1,0:T(4,128)(2,1)}, bf16[4,131072]{1,0:T(4,128)(2,1)S(1)}, u32[]{:S(2)}, u32[]{:S(2)}) collective-permute-start(bf16[4,131072]{1,0:T(4,128)(2,1)} %get-tuple-element.10), channel_id=1, source_target_pairs={{0,12},{1,13},{2,14},{3,15},{4,0},{5,1},{6,2},{7,3},{8,4},{9,5},{1... | collective-permute-start | bytes 3145736 | tf_op jit(solution)/shard_map/ppermute | solution.py:61
  235.9 10.8 %copy-start.3 = (bf16[1024,2,512]{2,1,0:T(2,128)(2,1)S(1)}, bf16[1024,2,512]{2,1,0:T(2,128)(2,1)}, u32[]{:S(2)}) copy-start(bf16[1024,2,512]{2,1,0:T(2,128)(2,1)} %reshape.236) | copy-start | bytes 6291460
  235.9 10.8 %copy-start.15 = (f32[2,1024,32,8]{1,2,3,0:T(8,128)S(1)}, f32[2,1024,32,8]{1,2,3,0:T(8,128)}, u32[]{:S(2)}) copy-start(f32[2,1024,32,8]{1,2,3,0:T(8,128)} %copy-done.14) | copy-start | bytes 6291460
  238.7 25.4 %collective-permute-start.10 = (f32[131072]{0:T(1024)}, f32[131072]{0:T(1024)S(1)}, u32[]{:S(2)}, u32[]{:S(2)}) collective-permute-start(f32[131072]{0:T(1024)} %bitcast.34), channel_id=1, source_target_pairs={{0,2},{1,3},{2,0},{3,1},{4,6},{5,7},{6,4},{7,5},{8,10},{9,11},{10,... | collective-permute-start | bytes 1572872 | tf_op jit(solution)/shard_map/ppermute | solution.py:67
  241.2 23.3 %collective-permute-start.11 = (f32[131072]{0:T(1024)}, f32[131072]{0:T(1024)S(1)}, u32[]{:S(2)}, u32[]{:S(2)}) collective-permute-start(f32[131072]{0:T(1024)} %bitcast.35), channel_id=1, source_target_pairs={{0,3},{1,0},{2,1},{3,2},{4,7},{5,4},{6,5},{7,6},{8,11},{9,8},{10,9... | collective-permute-start | bytes 1572872 | tf_op jit(solution)/shard_map/ppermute | solution.py:67
  244.0 23.4 %collective-permute-start.9 = (f32[131072]{0:T(1024)}, f32[131072]{0:T(1024)S(1)}, u32[]{:S(2)}, u32[]{:S(2)}) collective-permute-start(f32[131072]{0:T(1024)} %bitcast.33), channel_id=1, source_target_pairs={{0,1},{1,2},{2,3},{3,0},{4,5},{5,6},{6,7},{7,4},{8,9},{9,10},{10,1... | collective-permute-start | bytes 1572872 | tf_op jit(solution)/shard_map/ppermute | solution.py:67
  250.1 69.8 %all-to-all-start.1 = ((bf16[64,16,512]{2,1,0:T(8,128)(2,1)}), bf16[64,16,512]{2,1,0:T(8,128)(2,1)S(1)}, u32[]{:S(2)}, u32[]{:S(2)}) async-start(bf16[64,16,512]{2,1,0:T(8,128)(2,1)} %bitcast.18), calls=%async_computation.1 | async-start | bytes 2097152 | tf_op jit(solution)/shard_map/all_to_all | solution.py:136
  (7 other events, 17.7 us)

commit v2 on v1

--- a/solution.py
+++ b/solution.py
@@ -33,38 +33,59 @@
     return pairs
 
 
-def ring_gather(piece, rows, cols):
+def pick(pieces, index):
+    count = len(pieces)
+    out = []
+    for i in range(count):
+        chosen = pieces[count - 1]
+        for k in range(count - 2, -1, -1):
+            chosen = jnp.where((index - k) % count == i, pieces[k], chosen)
+        out.append(chosen)
+    return jnp.stack(out)
+
+
+def axis_gather(piece, rows, cols, along_cols):
+    count = rows * cols
+    f = lax.axis_index("fsdp")
+    size, index = (cols, f % cols) if along_cols else (rows, f // cols)
+    got = [piece] + [
+        lax.ppermute(piece, "fsdp", shift_pairs(count, rows, cols, s, along_cols)) for s in range(1, size)
+    ]
+    return pick(got, index)
+
+
+def grid_gather(piece, rows, cols, cols_first):
+    if cols_first:
+        line = axis_gather(piece, rows, cols, True)
+        return axis_gather(line, rows, cols, False)
+    line = axis_gather(piece, rows, cols, False)
+    return jnp.swapaxes(axis_gather(line, rows, cols, True), 0, 1)
+
+
+def grid_reduce_scatter(parts, rows, cols, rows_first):
     count = rows * cols
     f = lax.axis_index("fsdp")
     r, c = f // cols, f % cols
-    got = [piece] + [
-        lax.ppermute(piece, "fsdp", shift_pairs(count, rows, cols, s, True)) for s in range(1, cols)
-    ]
-    rev = jnp.stack([got[(-k) % cols] for k in range(cols)])
-    row = jnp.roll(rev, c, axis=0)
-    got = [row] + [
-        lax.ppermute(row, "fsdp", shift_pairs(count, rows, cols, s, False)) for s in range(1, rows)
-    ]
-    rev = jnp.stack([got[(-k) % rows] for k in range(rows)])
-    whole = jnp.roll(rev, r, axis=0)
-    return whole.reshape(count, piece.shape[0])
-
-
-def ring_reduce_scatter(chunks, rows, cols):
-    count = rows * cols
-    f = lax.axis_index("fsdp")
-    r, c = f // cols, f % cols
-    grid = chunks.reshape(rows, cols, chunks.shape[1])
-    total = lax.dynamic_index_in_dim(grid, r, 0, keepdims=False).astype(jnp.float32)
+    if rows_first:
+        total = lax.dynamic_index_in_dim(parts, r, 0, keepdims=False).astype(jnp.float32)
+        for s in range(1, rows):
+            part = lax.dynamic_index_in_dim(parts, (r + s) % rows, 0, keepdims=False)
+            got = lax.ppermute(part, "fsdp", shift_pairs(count, rows, cols, s, False))
+            total = total + got.astype(jnp.float32)
+        mine = lax.dynamic_index_in_dim(total, c, 0, keepdims=False)
+        for s in range(1, cols):
+            part = lax.dynamic_index_in_dim(total, (c + s) % cols, 0, keepdims=False)
+            mine = mine + lax.ppermute(part, "fsdp", shift_pairs(count, rows, cols, s, True))
+        return mine
+    total = lax.dynamic_index_in_dim(parts, c, 1, keepdims=False).astype(jnp.float32)
+    for s in range(1, cols):
+        part = lax.dynamic_index_in_dim(parts, (c + s) % cols, 1, keepdims=False)
+        got = lax.ppermute(part, "fsdp", shift_pairs(count, rows, cols, s, True))
+        total = total + got.astype(jnp.float32)
+    mine = lax.dynamic_index_in_dim(total, r, 0, keepdims=False)
     for s in range(1, rows):
-        part = lax.dynamic_index_in_dim(grid, (r + s) % rows, 0, keepdims=False)
-        total = total + lax.ppermute(part, "fsdp", shift_pairs(count, rows, cols, s, False)).astype(
-            jnp.float32
-        )
-    mine = lax.dynamic_index_in_dim(total, c, 0, keepdims=False)
-    for s in range(1, cols):
-        part = lax.dynamic_index_in_dim(total, (c + s) % cols, 0, keepdims=False)
-        mine = mine + lax.ppermute(part, "fsdp", shift_pairs(count, rows, cols, s, True))
+        part = lax.dynamic_index_in_dim(total, (r + s) % rows, 0, keepdims=False)
+        mine = mine + lax.ppermute(part, "fsdp", shift_pairs(count, rows, cols, s, False))
     return mine
 
 
@@ -80,11 +101,13 @@
     capacity = max(2, 4 * row_count // experts_all)
     assigned = 2 * row_count
 
-    in_size = weight_in.size
-    pieces = jnp.concatenate([weight_in.reshape(-1), weight_out.reshape(-1)])
-    gathered = ring_gather(pieces, rows, cols)
-    full_in = gathered[:, :in_size].reshape((fsdp_count * weight_in.shape[0],) + weight_in.shape[1:])
-    full_out = gathered[:, in_size:].reshape((fsdp_count * weight_out.shape[0],) + weight_out.shape[1:])
+    shard_in, shard_out = weight_in.shape[0], weight_out.shape[0]
+    full_in = grid_gather(weight_in, rows, cols, True).reshape(
+        (fsdp_count * shard_in,) + weight_in.shape[1:]
+    )
+    full_out = grid_gather(weight_out, rows, cols, False).reshape(
+        (fsdp_count * shard_out,) + weight_out.shape[1:]
+    )
 
     flat_ids = expert_ids.reshape(assigned)
     onehot = (flat_ids[:, None] == jnp.arange(experts_all, dtype=jnp.int32)[None, :]).astype(
@@ -122,12 +145,12 @@
     part_out = jnp.einsum(
         "sech,secd->hed", hidden, grad_rows, preferred_element_type=jnp.float32
     ).astype(jnp.bfloat16)
-    chunks = jnp.concatenate(
-        [part_in.reshape(fsdp_count, -1), part_out.reshape(fsdp_count, -1)], axis=1
-    )
-    summed = ring_reduce_scatter(chunks, rows, cols).astype(jnp.bfloat16)
-    grad_in = summed[:in_size].reshape(weight_in.shape)
-    grad_out = summed[in_size:].reshape(weight_out.shape)
+    grad_in = grid_reduce_scatter(
+        part_in.reshape((rows, cols, shard_in) + weight_in.shape[1:]), rows, cols, True
+    ).astype(jnp.bfloat16)
+    grad_out = grid_reduce_scatter(
+        part_out.reshape((rows, cols, shard_out) + weight_out.shape[1:]), rows, cols, False
+    ).astype(jnp.bfloat16)
 
     returned = jnp.einsum("sech,deh->secd", inner, full_in, preferred_element_type=jnp.float32)
     back = jnp.concatenate(

time: 327 us -> 213 us (0.65)
  waiting for transfers between devices: 144 us -> 48.8 us
  local copies, waits for them, and re-layouts: 92.6 us -> 23 us
  starting transfers between devices: 70.4 us -> 96.4 us
  other arithmetic: 8.22 us -> 29.5 us
    ppermute x12 -> x24, waiting for transfers between devices: 92.9 us -> 34.7 us  [the longest x12 15.5 us: axis_gather(): lax.ppermute(piece, 'fsdp', shift_pairs(count, rows, cols, s, along_cols))]
    all_to_all x1, waiting for transfers between devices: 50.9 us -> 0.01 us  [on_device(): lax.all_to_all(back, 'expert', split_axis=0, concat_axis=0, tiled=True)]
    ppermute x12 -> x24, starting transfers between devices: 40.2 us -> 74.1 us  [the longest x12 38 us: axis_gather(): lax.ppermute(piece, 'fsdp', shift_pairs(count, rows, cols, s, along_cols))]
    concatenate x6 -> x0, local copies, waits for them, and re-layouts: 19.7 us -> none  [the longest x1 10.3 us: ring_gather(): row = jnp.roll(rev, c, axis=0)]
    unnamed x45 -> x27, local copies, waits for them, and re-layouts: 18.2 us -> 3.37 us
    another operation x2 -> x9, other arithmetic: 0.65 us -> 15.2 us  [the longest x7 14.6 us: pick(): return jnp.stack(out)]
    all_to_all x1, waiting for transfers between devices: 0.01 us -> 14.1 us  [on_device(): lax.all_to_all(send, 'expert', split_axis=0, concat_axis=0, tiled=True)]
    reshape x3 -> x0, local copies, waits for them, and re-layouts: 10.9 us -> none  [the longest x1 4.06 us: ring_gather(): return whole.reshape(count, piece.shape[0])]
  transfers between devices with their start and end apart: 14 -> 26, of which waited for: 8 -> 10; matrix products, arithmetic and copies ran while one was open for 15% -> 24% of each run, Pallas kernels for 0% -> 0%
where the time goes in v2:
time: 213 us; the launch traced here: 209 us
  starting transfers between devices  96.4 us (45%)
  waiting for transfers between devices  48.8 us (23%)
  other arithmetic  29.5 us (14%)
  local copies, waits for them, and re-layouts  23 us (11%)
  matrix products  9.87 us (5%)
    ppermute x12, starting transfers between devices, axis_gather(): lax.ppermute(piece, 'fsdp', shift_pairs(count, rows, cols, s, along_cols))  38 us
    all_to_all x1, starting transfers between devices, on_device(): lax.all_to_all(send, 'expert', split_axis=0, concat_axis=0, tiled=True)  18.2 us
    ppermute x12, waiting for transfers between devices, axis_gather(): lax.ppermute(piece, 'fsdp', shift_pairs(count, rows, cols, s, along_cols))  15.5 us
    another operation x7, other arithmetic, pick(): return jnp.stack(out)  14.6 us
    all_to_all x1, waiting for transfers between devices, on_device(): lax.all_to_all(send, 'expert', split_axis=0, concat_axis=0, tiled=True)  14.1 us
    ppermute x3, starting transfers between devices, grid_reduce_scatter(): got = lax.ppermute(part, 'fsdp', shift_pairs(count, rows, cols, s, False))  12.5 us
    ppermute x3, waiting for transfers between devices, grid_reduce_scatter(): got = lax.ppermute(part, 'fsdp', shift_pairs(count, rows, cols, s, True))  10.1 us
    ppermute x3, starting transfers between devices, grid_reduce_scatter(): lax.ppermute(part, 'fsdp', shift_pairs(count, rows, cols, s, False))  8.41 us
  transfers between devices with their start and end apart: 26, of which 10 were waited for; matrix products, arithmetic and copies ran while one was open for 24% of the time, Pallas kernels for 0%

profile of v2, /device:TPU:1, one launch (start us, length us, event | category | flops | bytes accessed | tf_op | source)
XLA Modules:
  0.0 209.4 jit_solution(17380907768618204428)
XLA Ops:
  0.6 5.6 %collective-permute-start.7 = (bf16[32,2,1024]{2,1,0:T(2,128)(2,1)}, bf16[32,2,1024]{2,1,0:T(2,128)(2,1)S(1)}, u32[]{:S(2)}, u32[]{:S(2)}) collective-permute-start(bf16[32,2,1024]{2,1,0:T(2,128)(2,1)} %param.12), channel_id=1, source_target_pairs={{0,2},{1,3},{2,0},{3,1},{4,6},{5,7},{6,4},{7,5},{8,10},{9,11},{10,... | collective-permute-start | bytes 393224 | tf_op jit(solution)/shard_map/ppermute | solution.py:52
  8.5 4.3 %collective-permute-start.8 = (bf16[32,2,1024]{2,1,0:T(2,128)(2,1)}, bf16[32,2,1024]{2,1,0:T(2,128)(2,1)S(1)}, u32[]{:S(2)}, u32[]{:S(2)}) collective-permute-start(bf16[32,2,1024]{2,1,0:T(2,128)(2,1)} %param.12), channel_id=1, source_target_pairs={{0,3},{1,0},{2,1},{3,2},{4,7},{5,4},{6,5},{7,6},{8,11},{9,8},{10,9... | collective-permute-start | bytes 393224 | tf_op jit(solution)/shard_map/ppermute | solution.py:52
  12.8 4.8 %collective-permute-start.1 = (bf16[64,2,512]{2,1,0:T(2,128)(2,1)}, bf16[64,2,512]{2,1,0:T(2,128)(2,1)S(1)}, u32[]{:S(2)}, u32[]{:S(2)}) collective-permute-start(bf16[64,2,512]{2,1,0:T(2,128)(2,1)} %param.13), channel_id=1, source_target_pairs={{0,8},{1,9},{2,10},{3,11},{4,12},{5,13},{6,14},{7,15},{8,0},{9,1},... | collective-permute-start | bytes 393224 | tf_op jit(solution)/shard_map/ppermute | solution.py:52
  31.0 4.2 %collective-permute-start.2 = (bf16[64,2,512]{2,1,0:T(2,128)(2,1)S(1)}, bf16[64,2,512]{2,1,0:T(2,128)(2,1)}, u32[]{:S(2)}, u32[]{:S(2)}) collective-permute-start(bf16[64,2,512]{2,1,0:T(2,128)(2,1)S(1)} %copy-done.9), channel_id=1, source_target_pairs={{0,12},{1,13},{2,14},{3,15},{4,0},{5,1},{6,2},{7,3},{8,4},{9,5},{1... | collective-permute-start | bytes 393224 | tf_op jit(solution)/shard_map/ppermute | solution.py:52
  39.5 2.9 %collective-permute-start.10 = (bf16[4,32,2,1024]{3,2,1,0:T(2,128)(2,1)}, bf16[4,32,2,1024]{3,2,1,0:T(2,128)(2,1)S(1)}, u32[]{:S(2)}, u32[]{:S(2)}) collective-permute-start(bf16[4,32,2,1024]{3,2,1,0:T(2,128)(2,1)} %pad_maximum_fusion.4), channel_id=1, source_target_pairs={{0,8},{1,9},{2,10},{3,11},{4,12},{5,13},{6,14},{7,15},{8,0},{9,1},... | collective-permute-start | bytes 1572872 | tf_op jit(solution)/shard_map/ppermute | solution.py:52
  46.0 18.2 %all-to-all-start = ((bf16[64,16,512]{2,1,0:T(8,128)(2,1)}), bf16[64,16,512]{2,1,0:T(8,128)(2,1)S(1)}, u32[]{:S(2)}, u32[]{:S(2)}) async-start(bf16[64,16,512]{2,1,0:T(8,128)(2,1)} %pad_maximum_fusion.1), calls=%async_computation | async-start | bytes 2097152 | tf_op jit(solution)/shard_map/all_to_all | solution.py:131
  74.2 2.9 %fusion.18 = (bf16[1,4,32,2,1024]{4,3,2,1,0:T(2,128)(2,1)S(1)}, bf16[1,4,32,2,1024]{4,3,2,1,0:T(2,128)(2,1)S(1)}, bf16[1,4,32,2,1024]{4,3,2,1,0:T(2,128)(2,1)S(1)}, bf16[1,4,32,2,1024]{4,3,2,1,0:T(2,128)(2,1)S(1)}) fusion(pred[]{:T(512)S(6)} %eq.190, bf16[4,32,2,1024]{3,2,1,0:T(2,128)(2,1)S(1)} %collective-permute-done.9, pred[]{:T(512)S(6)} %eq.191, ...), kind=kLoop, calls=%fused_computation.61 | loop fusion | flops 3932160 | bytes 4194316 | tf_op jit(solution)/shard_map/stack | solution.py:44
  77.1 3.9 %pad_maximum_fusion = bf16[4,4,32,2,1024]{4,3,2,1,0:T(2,128)(2,1)S(1)} fusion(bf16[1,4,32,2,1024]{4,3,2,1,0:T(2,128)(2,1)S(1)} %get-tuple-element.22, bf16[1,4,32,2,1024]{4,3,2,1,0:T(2,128)(2,1)S(1)} %get-tuple-element.23, bf16[1,4,32,2,1024]{4,3,2,1,0:T(2,128)(2,1)S(1)} %get-tuple-element.24, bf16[1,4,32,2,1024]{4,3,2,1,0:T(2,128)(2,1)S(1)} %get-tuple-element.21), kind=kLoop, calls=%fused_computation.8 | loop fusion | flops 3145728 | bytes 4194304 | tf_op jit(solution)/shard_map/stack | solution.py:44
  81.9 3.5 %collective-permute-done.4 = bf16[4,64,2,512]{3,2,1,0:T(2,128)(2,1)S(1)} collective-permute-done((bf16[4,64,2,512]{3,2,1,0:T(2,128)(2,1)S(1)}, bf16[4,64,2,512]{3,2,1,0:T(2,128)(2,1)S(1)}, u32[]{:S(2)}, u32[]{:S(2)}) %collective-permute-start.4) | collective-permute-done | bytes 524320 | tf_op jit(solution)/shard_map/ppermute | solution.py:52
  85.3 11.8 %collective-permute-done.3 = bf16[4,64,2,512]{3,2,1,0:T(2,128)(2,1)S(1)} collective-permute-done((bf16[4,64,2,512]{3,2,1,0:T(2,128)(2,1)S(1)}, bf16[4,64,2,512]{3,2,1,0:T(2,128)(2,1)S(1)}, u32[]{:S(2)}, u32[]{:S(2)}) %collective-permute-start.3) | collective-permute-done | bytes 524320 | tf_op jit(solution)/shard_map/ppermute | solution.py:52
  97.1 2.9 %fusion.14 = (bf16[1,4,64,2,512]{4,3,2,1,0:T(2,128)(2,1)S(1)}, bf16[1,4,64,2,512]{4,3,2,1,0:T(2,128)(2,1)S(1)}, bf16[1,4,64,2,512]{4,3,2,1,0:T(2,128)(2,1)S(1)}, bf16[1,4,64,2,512]{4,3,2,1,0:T(2,128)(2,1)S(1)}) fusion(pred[]{:T(512)S(6)} %eq.189, bf16[4,64,2,512]{3,2,1,0:T(2,128)(2,1)S(1)} %collective-permute-done.3, pred[]{:T(512)S(6)} %eq.202, ...), kind=kLoop, calls=%fused_computation.57 | loop fusion | flops 3932160 | bytes 4194316 | tf_op jit(solution)/shard_map/stack | solution.py:44
  100.1 3.9 %maximum_bitcast_fusion = bf16[4,4,64,2,512]{4,3,2,0,1:T(2,128)(2,1)S(1)} fusion(bf16[1,4,64,2,512]{4,3,2,1,0:T(2,128)(2,1)S(1)} %get-tuple-element.18, bf16[1,4,64,2,512]{4,3,2,1,0:T(2,128)(2,1)S(1)} %get-tuple-element.19, bf16[1,4,64,2,512]{4,3,2,1,0:T(2,128)(2,1)S(1)} %get-tuple-element.20, bf16[1,4,64,2,512]{4,3,2,1,0:T(2,128)(2,1)S(1)} %get-tuple-element.17), kind=kLoop, calls=%fused_computation.7 | loop fusion | flops 3145728 | bytes 4194304 | tf_op jit(solution)/shard_map/transpose | solution.py:62
  105.7 14.1 %all-to-all-done = bf16[64,16,512]{2,1,0:T(8,128)(2,1)S(1)} async-done(((bf16[64,16,512]{2,1,0:T(8,128)(2,1)}), bf16[64,16,512]{2,1,0:T(8,128)(2,1)S(1)}, u32[]{:S(2)}, u32[]{:S(2)}) %all-to-all-start) | async-done | bytes 1048608 | tf_op jit(solution)/shard_map/all_to_all | solution.py:131
  127.0 4.1 %all-to-all-start.1 = ((bf16[64,16,512]{2,1,0:T(8,128)(2,1)}), bf16[64,16,512]{2,1,0:T(8,128)(2,1)S(1)}, u32[]{:S(2)}, u32[]{:S(2)}) async-start(bf16[64,16,512]{2,1,0:T(8,128)(2,1)} %bitcast.37), calls=%async_computation.1 | async-start | bytes 2097152 | tf_op jit(solution)/shard_map/all_to_all | solution.py:159
  131.2 4.0 %fusion.7 = bf16[1024,2,512]{0,2,1:T(8,128)(2,1)} fusion(bf16[32,2,8,512]{3,2,1,0:T(8,128)(2,1)S(1)} %copy-done.5, f32[2,1024,32,8]{1,2,3,0:T(8,128)} %copy-done.11), kind=kOutput, calls=%fused_computation.20 | convolution fusion | flops 540540928 | bytes 4718592 | tf_op jit(solution)/shard_map/sech,secd->hed/dot_general | solution.py:145
  135.2 2.9 %copy.59 = bf16[1024,2,512]{2,0,1:T(8,128)(2,1)S(1)} copy(bf16[1024,2,512]{0,2,1:T(8,128)(2,1)} %fusion.7) | data formatting | bytes 4194304 | tf_op jit(solution)/shard_map/convert_element_type | solution.py:147
  141.3 4.6 %collective-permute-start.20 = (bf16[4,64,2,512]{3,1,0,2:T(8,128)(2,1)}, bf16[4,64,2,512]{3,1,0,2:T(8,128)(2,1)S(1)}, u32[]{:S(2)}, u32[]{:S(2)}) collective-permute-start(bf16[4,64,2,512]{3,1,0,2:T(8,128)(2,1)} %get-tuple-element.12), channel_id=1, source_target_pairs={{0,3},{1,0},{2,1},{3,2},{4,7},{5,4},{6,5},{7,6},{8,11},{9,8},{10,9... | collective-permute-start | bytes 1572872 | tf_op jit(solution)/shard_map/ppermute | solution.py:83
  150.2 3.3 %collective-permute-start.12 = (bf16[4,32,2,1024]{3,1,0,2:T(8,128)(2,1)S(1)}, bf16[4,32,2,1024]{3,1,0,2:T(8,128)(2,1)S(1)}, u32[]{:S(2)}, u32[]{:S(2)}) collective-permute-start(bf16[4,32,2,1024]{3,1,0,2:T(8,128)(2,1)S(1)} %get-tuple-element.14), channel_id=1, source_target_pairs={{0,4},{1,5},{2,6},{3,7},{4,8},{5,9},{6,10},{7,11},{8,12},{9,13},{1... | collective-permute-start | bytes 1572872 | tf_op jit(solution)/shard_map/ppermute | solution.py:73
  153.5 3.4 %collective-permute-start.14 = (bf16[4,32,2,1024]{3,1,0,2:T(8,128)(2,1)S(1)}, bf16[4,32,2,1024]{3,1,0,2:T(8,128)(2,1)S(1)}, u32[]{:S(2)}, u32[]{:S(2)}) collective-permute-start(bf16[4,32,2,1024]{3,1,0,2:T(8,128)(2,1)S(1)} %get-tuple-element.15), channel_id=1, source_target_pairs={{0,12},{1,13},{2,14},{3,15},{4,0},{5,1},{6,2},{7,3},{8,4},{9,5},{1... | collective-permute-start | bytes 1572872 | tf_op jit(solution)/shard_map/ppermute | solution.py:73
  157.0 10.1 %collective-permute-done.18 = bf16[4,64,2,512]{3,1,0,2:T(8,128)(2,1)} collective-permute-done((bf16[4,64,2,512]{3,1,0,2:T(8,128)(2,1)}, bf16[4,64,2,512]{3,1,0,2:T(8,128)(2,1)}, u32[]{:S(2)}, u32[]{:S(2)}) %collective-permute-start.18) | collective-permute-done | bytes 524320 | tf_op jit(solution)/shard_map/ppermute | solution.py:83
  167.1 5.7 %collective-permute-start.13 = (bf16[4,32,2,1024]{3,1,0,2:T(8,128)(2,1)S(1)}, bf16[4,32,2,1024]{3,1,0,2:T(8,128)(2,1)S(1)}, u32[]{:S(2)}, u32[]{:S(2)}) collective-permute-start(bf16[4,32,2,1024]{3,1,0,2:T(8,128)(2,1)S(1)} %get-tuple-element.16), channel_id=1, source_target_pairs={{0,8},{1,9},{2,10},{3,11},{4,12},{5,13},{6,14},{7,15},{8,0},{9,1},... | collective-permute-start | bytes 1572872 | tf_op jit(solution)/shard_map/ppermute | solution.py:73
  176.2 4.6 %collective-permute-start.23 = (f32[64,2,512]{2,0,1:T(8,128)S(1)}, f32[64,2,512]{2,0,1:T(8,128)S(1)}, u32[]{:S(2)}, u32[]{:S(2)}) collective-permute-start(f32[64,2,512]{2,0,1:T(8,128)S(1)} %get-tuple-element.26), channel_id=1, source_target_pairs={{0,12},{1,13},{2,14},{3,15},{4,0},{5,1},{6,2},{7,3},{8,4},{9,5},{1... | collective-permute-start | bytes 786440 | tf_op jit(solution)/shard_map/ppermute | solution.py:88
  187.0 3.0 %collective-permute-start.16 = (f32[32,2,1024]{2,1,0:T(2,128)S(1)}, f32[32,2,1024]{2,1,0:T(2,128)}, u32[]{:S(2)}, u32[]{:S(2)}) collective-permute-start(f32[32,2,1024]{2,1,0:T(2,128)S(1)} %bitcast.188), channel_id=1, source_target_pairs={{0,2},{1,3},{2,0},{3,1},{4,6},{5,7},{6,4},{7,5},{8,10},{9,11},{10,... | collective-permute-start | bytes 786440 | tf_op jit(solution)/shard_map/ppermute | solution.py:78
  198.8 2.9 %collective-permute-done.17 = f32[32,2,1024]{2,1,0:T(2,128)} collective-permute-done((f32[32,2,1024]{2,1,0:T(2,128)S(1)}, f32[32,2,1024]{2,1,0:T(2,128)}, u32[]{:S(2)}, u32[]{:S(2)}) %collective-permute-start.17) | collective-permute-done | bytes 262176 | tf_op jit(solution)/shard_map/ppermute | solution.py:78
  (123 shorter events, 76.1 us)
Async XLA Ops:
  0.6 30.3 %collective-permute-start.7 = (bf16[32,2,1024]{2,1,0:T(2,128)(2,1)}, bf16[32,2,1024]{2,1,0:T(2,128)(2,1)S(1)}, u32[]{:S(2)}, u32[]{:S(2)}) collective-permute-start(bf16[32,2,1024]{2,1,0:T(2,128)(2,1)} %param.12), channel_id=1, source_target_pairs={{0,2},{1,3},{2,0},{3,1},{4,6},{5,7},{6,4},{7,5},{8,10},{9,11},{10,... | collective-permute-start | bytes 393224 | tf_op jit(solution)/shard_map/ppermute | solution.py:52
  6.3 28.9 %collective-permute-start.6 = (bf16[32,2,1024]{2,1,0:T(2,128)(2,1)}, bf16[32,2,1024]{2,1,0:T(2,128)(2,1)S(1)}, u32[]{:S(2)}, u32[]{:S(2)}) collective-permute-start(bf16[32,2,1024]{2,1,0:T(2,128)(2,1)} %param.12), channel_id=1, source_target_pairs={{0,1},{1,2},{2,3},{3,0},{4,5},{5,6},{6,7},{7,4},{8,9},{9,10},{10,1... | collective-permute-start | bytes 393224 | tf_op jit(solution)/shard_map/ppermute | solution.py:52
  8.5 26.7 %collective-permute-start.8 = (bf16[32,2,1024]{2,1,0:T(2,128)(2,1)}, bf16[32,2,1024]{2,1,0:T(2,128)(2,1)S(1)}, u32[]{:S(2)}, u32[]{:S(2)}) collective-permute-start(bf16[32,2,1024]{2,1,0:T(2,128)(2,1)} %param.12), channel_id=1, source_target_pairs={{0,3},{1,0},{2,1},{3,2},{4,7},{5,4},{6,5},{7,6},{8,11},{9,8},{10,9... | collective-permute-start | bytes 393224 | tf_op jit(solution)/shard_map/ppermute | solution.py:52
  12.8 29.6 %collective-permute-start.1 = (bf16[64,2,512]{2,1,0:T(2,128)(2,1)}, bf16[64,2,512]{2,1,0:T(2,128)(2,1)S(1)}, u32[]{:S(2)}, u32[]{:S(2)}) collective-permute-start(bf16[64,2,512]{2,1,0:T(2,128)(2,1)} %param.13), channel_id=1, source_target_pairs={{0,8},{1,9},{2,10},{3,11},{4,12},{5,13},{6,14},{7,15},{8,0},{9,1},... | collective-permute-start | bytes 393224 | tf_op jit(solution)/shard_map/ppermute | solution.py:52
  17.6 46.6 %collective-permute-start = (bf16[64,2,512]{2,1,0:T(2,128)(2,1)}, bf16[64,2,512]{2,1,0:T(2,128)(2,1)S(1)}, u32[]{:S(2)}, u32[]{:S(2)}) collective-permute-start(bf16[64,2,512]{2,1,0:T(2,128)(2,1)} %param.13), channel_id=1, source_target_pairs={{0,4},{1,5},{2,6},{3,7},{4,8},{5,9},{6,10},{7,11},{8,12},{9,13},{1... | collective-permute-start | bytes 393224 | tf_op jit(solution)/shard_map/ppermute | solution.py:52
  31.0 33.2 %collective-permute-start.2 = (bf16[64,2,512]{2,1,0:T(2,128)(2,1)S(1)}, bf16[64,2,512]{2,1,0:T(2,128)(2,1)}, u32[]{:S(2)}, u32[]{:S(2)}) collective-permute-start(bf16[64,2,512]{2,1,0:T(2,128)(2,1)S(1)} %copy-done.9), channel_id=1, source_target_pairs={{0,12},{1,13},{2,14},{3,15},{4,0},{5,1},{6,2},{7,3},{8,4},{9,5},{1... | collective-permute-start | bytes 393224 | tf_op jit(solution)/shard_map/ppermute | solution.py:52
  37.6 33.8 %collective-permute-start.11 = (bf16[4,32,2,1024]{3,2,1,0:T(2,128)(2,1)}, bf16[4,32,2,1024]{3,2,1,0:T(2,128)(2,1)S(1)}, u32[]{:S(2)}, u32[]{:S(2)}) collective-permute-start(bf16[4,32,2,1024]{3,2,1,0:T(2,128)(2,1)} %pad_maximum_fusion.4), channel_id=1, source_target_pairs={{0,12},{1,13},{2,14},{3,15},{4,0},{5,1},{6,2},{7,3},{8,4},{9,5},{1... | collective-permute-start | bytes 1572872 | tf_op jit(solution)/shard_map/ppermute | solution.py:52
  39.5 34.6 %collective-permute-start.10 = (bf16[4,32,2,1024]{3,2,1,0:T(2,128)(2,1)}, bf16[4,32,2,1024]{3,2,1,0:T(2,128)(2,1)S(1)}, u32[]{:S(2)}, u32[]{:S(2)}) collective-permute-start(bf16[4,32,2,1024]{3,2,1,0:T(2,128)(2,1)} %pad_maximum_fusion.4), channel_id=1, source_target_pairs={{0,8},{1,9},{2,10},{3,11},{4,12},{5,13},{6,14},{7,15},{8,0},{9,1},... | collective-permute-start | bytes 1572872 | tf_op jit(solution)/shard_map/ppermute | solution.py:52
  42.4 31.8 %collective-permute-start.9 = (bf16[4,32,2,1024]{3,2,1,0:T(2,128)(2,1)}, bf16[4,32,2,1024]{3,2,1,0:T(2,128)(2,1)S(1)}, u32[]{:S(2)}, u32[]{:S(2)}) collective-permute-start(bf16[4,32,2,1024]{3,2,1,0:T(2,128)(2,1)} %pad_maximum_fusion.4), channel_id=1, source_target_pairs={{0,4},{1,5},{2,6},{3,7},{4,8},{5,9},{6,10},{7,11},{8,12},{9,13},{1... | collective-permute-start | bytes 1572872 | tf_op jit(solution)/shard_map/ppermute | solution.py:52
  46.0 73.9 %all-to-all-start = ((bf16[64,16,512]{2,1,0:T(8,128)(2,1)}), bf16[64,16,512]{2,1,0:T(8,128)(2,1)S(1)}, u32[]{:S(2)}, u32[]{:S(2)}) async-start(bf16[64,16,512]{2,1,0:T(8,128)(2,1)} %pad_maximum_fusion.1), calls=%async_computation | async-start | bytes 2097152 | tf_op jit(solution)/shard_map/all_to_all | solution.py:131
  66.7 15.1 %collective-permute-start.5 = (bf16[4,64,2,512]{3,2,1,0:T(2,128)(2,1)S(1)}, bf16[4,64,2,512]{3,2,1,0:T(2,128)(2,1)S(1)}, u32[]{:S(2)}, u32[]{:S(2)}) collective-permute-start(bf16[4,64,2,512]{3,2,1,0:T(2,128)(2,1)S(1)} %pad_maximum_fusion.3), channel_id=1, source_target_pairs={{0,3},{1,0},{2,1},{3,2},{4,7},{5,4},{6,5},{7,6},{8,11},{9,8},{10,9... | collective-permute-start | bytes 1572872 | tf_op jit(solution)/shard_map/ppermute | solution.py:52
  68.6 16.7 %collective-permute-start.4 = (bf16[4,64,2,512]{3,2,1,0:T(2,128)(2,1)S(1)}, bf16[4,64,2,512]{3,2,1,0:T(2,128)(2,1)S(1)}, u32[]{:S(2)}, u32[]{:S(2)}) collective-permute-start(bf16[4,64,2,512]{3,2,1,0:T(2,128)(2,1)S(1)} %pad_maximum_fusion.3), channel_id=1, source_target_pairs={{0,2},{1,3},{2,0},{3,1},{4,6},{5,7},{6,4},{7,5},{8,10},{9,11},{10,... | collective-permute-start | bytes 1572872 | tf_op jit(solution)/shard_map/ppermute | solution.py:52
  71.5 25.7 %collective-permute-start.3 = (bf16[4,64,2,512]{3,2,1,0:T(2,128)(2,1)S(1)}, bf16[4,64,2,512]{3,2,1,0:T(2,128)(2,1)S(1)}, u32[]{:S(2)}, u32[]{:S(2)}) collective-permute-start(bf16[4,64,2,512]{3,2,1,0:T(2,128)(2,1)S(1)} %pad_maximum_fusion.3), channel_id=1, source_target_pairs={{0,1},{1,2},{2,3},{3,0},{4,5},{5,6},{6,7},{7,4},{8,9},{9,10},{10,1... | collective-permute-start | bytes 1572872 | tf_op jit(solution)/shard_map/ppermute | solution.py:52
  127.0 76.8 %all-to-all-start.1 = ((bf16[64,16,512]{2,1,0:T(8,128)(2,1)}), bf16[64,16,512]{2,1,0:T(8,128)(2,1)S(1)}, u32[]{:S(2)}, u32[]{:S(2)}) async-start(bf16[64,16,512]{2,1,0:T(8,128)(2,1)} %bitcast.37), calls=%async_computation.1 | async-start | bytes 2097152 | tf_op jit(solution)/shard_map/all_to_all | solution.py:159
  139.3 27.8 %collective-permute-start.18 = (bf16[4,64,2,512]{3,1,0,2:T(8,128)(2,1)}, bf16[4,64,2,512]{3,1,0,2:T(8,128)(2,1)}, u32[]{:S(2)}, u32[]{:S(2)}) collective-permute-start(bf16[4,64,2,512]{3,1,0,2:T(8,128)(2,1)} %get-tuple-element.11), channel_id=1, source_target_pairs={{0,1},{1,2},{2,3},{3,0},{4,5},{5,6},{6,7},{7,4},{8,9},{9,10},{10,1... | collective-permute-start | bytes 1572872 | tf_op jit(solution)/shard_map/ppermute | solution.py:83
  141.3 31.5 %collective-permute-start.20 = (bf16[4,64,2,512]{3,1,0,2:T(8,128)(2,1)}, bf16[4,64,2,512]{3,1,0,2:T(8,128)(2,1)S(1)}, u32[]{:S(2)}, u32[]{:S(2)}) collective-permute-start(bf16[4,64,2,512]{3,1,0,2:T(8,128)(2,1)} %get-tuple-element.12), channel_id=1, source_target_pairs={{0,3},{1,0},{2,1},{3,2},{4,7},{5,4},{6,5},{7,6},{8,11},{9,8},{10,9... | collective-permute-start | bytes 1572872 | tf_op jit(solution)/shard_map/ppermute | solution.py:83
  145.9 27.0 %collective-permute-start.19 = (bf16[4,64,2,512]{3,1,0,2:T(8,128)(2,1)}, bf16[4,64,2,512]{3,1,0,2:T(8,128)(2,1)S(1)}, u32[]{:S(2)}, u32[]{:S(2)}) collective-permute-start(bf16[4,64,2,512]{3,1,0,2:T(8,128)(2,1)} %get-tuple-element.13), channel_id=1, source_target_pairs={{0,2},{1,3},{2,0},{3,1},{4,6},{5,7},{6,4},{7,5},{8,10},{9,11},{10,... | collective-permute-start | bytes 1572872 | tf_op jit(solution)/shard_map/ppermute | solution.py:83
  150.2 30.5 %collective-permute-start.12 = (bf16[4,32,2,1024]{3,1,0,2:T(8,128)(2,1)S(1)}, bf16[4,32,2,1024]{3,1,0,2:T(8,128)(2,1)S(1)}, u32[]{:S(2)}, u32[]{:S(2)}) collective-permute-start(bf16[4,32,2,1024]{3,1,0,2:T(8,128)(2,1)S(1)} %get-tuple-element.14), channel_id=1, source_target_pairs={{0,4},{1,5},{2,6},{3,7},{4,8},{5,9},{6,10},{7,11},{8,12},{9,13},{1... | collective-permute-start | bytes 1572872 | tf_op jit(solution)/shard_map/ppermute | solution.py:73
  153.5 29.2 %collective-permute-start.14 = (bf16[4,32,2,1024]{3,1,0,2:T(8,128)(2,1)S(1)}, bf16[4,32,2,1024]{3,1,0,2:T(8,128)(2,1)S(1)}, u32[]{:S(2)}, u32[]{:S(2)}) collective-permute-start(bf16[4,32,2,1024]{3,1,0,2:T(8,128)(2,1)S(1)} %get-tuple-element.15), channel_id=1, source_target_pairs={{0,12},{1,13},{2,14},{3,15},{4,0},{5,1},{6,2},{7,3},{8,4},{9,5},{1... | collective-permute-start | bytes 1572872 | tf_op jit(solution)/shard_map/ppermute | solution.py:73
  167.1 16.9 %collective-permute-start.13 = (bf16[4,32,2,1024]{3,1,0,2:T(8,128)(2,1)S(1)}, bf16[4,32,2,1024]{3,1,0,2:T(8,128)(2,1)S(1)}, u32[]{:S(2)}, u32[]{:S(2)}) collective-permute-start(bf16[4,32,2,1024]{3,1,0,2:T(8,128)(2,1)S(1)} %get-tuple-element.16), channel_id=1, source_target_pairs={{0,8},{1,9},{2,10},{3,11},{4,12},{5,13},{6,14},{7,15},{8,0},{9,1},... | collective-permute-start | bytes 1572872 | tf_op jit(solution)/shard_map/ppermute | solution.py:73
  174.3 17.8 %collective-permute-start.21 = (f32[64,2,512]{2,0,1:T(8,128)S(1)}, f32[64,2,512]{2,0,1:T(8,128)S(1)}, u32[]{:S(2)}, u32[]{:S(2)}) collective-permute-start(f32[64,2,512]{2,0,1:T(8,128)S(1)} %get-tuple-element.25), channel_id=1, source_target_pairs={{0,4},{1,5},{2,6},{3,7},{4,8},{5,9},{6,10},{7,11},{8,12},{9,13},{1... | collective-permute-start | bytes 786440 | tf_op jit(solution)/shard_map/ppermute | solution.py:88
  176.2 17.9 %collective-permute-start.23 = (f32[64,2,512]{2,0,1:T(8,128)S(1)}, f32[64,2,512]{2,0,1:T(8,128)S(1)}, u32[]{:S(2)}, u32[]{:S(2)}) collective-permute-start(f32[64,2,512]{2,0,1:T(8,128)S(1)} %get-tuple-element.26), channel_id=1, source_target_pairs={{0,12},{1,13},{2,14},{3,15},{4,0},{5,1},{6,2},{7,3},{8,4},{9,5},{1... | collective-permute-start | bytes 786440 | tf_op jit(solution)/shard_map/ppermute | solution.py:88
  180.8 14.4 %collective-permute-start.22 = (f32[64,2,512]{2,0,1:T(8,128)S(1)}, f32[64,2,512]{2,0,1:T(8,128)S(1)}, u32[]{:S(2)}, u32[]{:S(2)}) collective-permute-start(f32[64,2,512]{2,0,1:T(8,128)S(1)} %get-tuple-element.27), channel_id=1, source_target_pairs={{0,8},{1,9},{2,10},{3,11},{4,12},{5,13},{6,14},{7,15},{8,0},{9,1},... | collective-permute-start | bytes 786440 | tf_op jit(solution)/shard_map/ppermute | solution.py:88
  185.0 12.0 %collective-permute-start.15 = (f32[32,2,1024]{2,1,0:T(2,128)S(1)}, f32[32,2,1024]{2,1,0:T(2,128)}, u32[]{:S(2)}, u32[]{:S(2)}) collective-permute-start(f32[32,2,1024]{2,1,0:T(2,128)S(1)} %bitcast.189), channel_id=1, source_target_pairs={{0,1},{1,2},{2,3},{3,0},{4,5},{5,6},{6,7},{7,4},{8,9},{9,10},{10,1... | collective-permute-start | bytes 786440 | tf_op jit(solution)/shard_map/ppermute | solution.py:78
  (14 other events, 93.4 us)

commit v3 on v2

--- a/solution.py
+++ b/solution.py
@@ -89,11 +89,10 @@
     return mine
 
 
-def on_device(states, rates, expert_ids, gate_weights, cotangent, weight_in, weight_out):
+def body(states, rates, expert_ids, gate_weights, cotangent, weight_in, weight_out):
     row_count = states.shape[0]
     feature = states.shape[1]
     local_count = weight_in.shape[1]
-    hidden_width = weight_in.shape[2]
     groups = lax.axis_size("expert")
     fsdp_count = lax.axis_size("fsdp")
     rows, cols = grid_of(fsdp_count)
@@ -102,13 +101,6 @@
     assigned = 2 * row_count
 
     shard_in, shard_out = weight_in.shape[0], weight_out.shape[0]
-    full_in = grid_gather(weight_in, rows, cols, True).reshape(
-        (fsdp_count * shard_in,) + weight_in.shape[1:]
-    )
-    full_out = grid_gather(weight_out, rows, cols, False).reshape(
-        (fsdp_count * shard_out,) + weight_out.shape[1:]
-    )
-
     flat_ids = expert_ids.reshape(assigned)
     onehot = (flat_ids[:, None] == jnp.arange(experts_all, dtype=jnp.int32)[None, :]).astype(
         jnp.int32
@@ -129,34 +121,36 @@
     send_grads = padded_descent[source].reshape(send_shape)
     send = jnp.concatenate([send_knots, send_grads], axis=1)
     got = lax.all_to_all(send, "expert", split_axis=0, concat_axis=0, tiled=True)
+    full_in = lax.all_gather(weight_in, "fsdp", axis=0, tiled=True)
+    full_out = grid_gather(weight_out, rows, cols, False).reshape(
+        (fsdp_count * shard_out,) + weight_out.shape[1:]
+    )
     got = got.reshape(groups, local_count, 2 * capacity, feature)
     knot_rows = got[:, :, :capacity]
     grad_rows = got[:, :, capacity:]
 
     preact = jnp.einsum("secd,deh->sech", knot_rows, full_in, preferred_element_type=jnp.float32)
     hidden = activate(preact).astype(jnp.bfloat16)
-    values = jnp.einsum("sech,hed->secd", hidden, full_out, preferred_element_type=jnp.float32)
-    slope = jnp.einsum("secd,hed->sech", grad_rows, full_out, preferred_element_type=jnp.float32)
-    inner = (slope * activate_slope(preact)).astype(jnp.bfloat16)
-
-    part_in = jnp.einsum(
-        "secd,sech->deh", knot_rows, inner, preferred_element_type=jnp.float32
-    ).astype(jnp.bfloat16)
     part_out = jnp.einsum(
         "sech,secd->hed", hidden, grad_rows, preferred_element_type=jnp.float32
-    ).astype(jnp.bfloat16)
-    grad_in = grid_reduce_scatter(
-        part_in.reshape((rows, cols, shard_in) + weight_in.shape[1:]), rows, cols, True
     ).astype(jnp.bfloat16)
     grad_out = grid_reduce_scatter(
         part_out.reshape((rows, cols, shard_out) + weight_out.shape[1:]), rows, cols, False
     ).astype(jnp.bfloat16)
-
+    values = jnp.einsum("sech,hed->secd", hidden, full_out, preferred_element_type=jnp.float32)
+    slope = jnp.einsum("secd,hed->sech", grad_rows, full_out, preferred_element_type=jnp.float32)
+    inner = (slope * activate_slope(preact)).astype(jnp.bfloat16)
     returned = jnp.einsum("sech,deh->secd", inner, full_in, preferred_element_type=jnp.float32)
     back = jnp.concatenate(
         [values.astype(jnp.bfloat16), returned.astype(jnp.bfloat16)], axis=2
     ).reshape(experts_all, 2 * capacity, feature)
     back = lax.all_to_all(back, "expert", split_axis=0, concat_axis=0, tiled=True)
+    part_in = jnp.einsum(
+        "secd,sech->deh", knot_rows, inner, preferred_element_type=jnp.float32
+    ).astype(jnp.bfloat16)
+    grad_in = grid_reduce_scatter(
+        part_in.reshape((rows, cols, shard_in) + weight_in.shape[1:]), rows, cols, True
+    ).astype(jnp.bfloat16)
     back = back.reshape(experts_all * capacity * 2, feature)
     values_knot = back[(position // capacity) * (2 * capacity) + position % capacity]
     values_knot = values_knot.reshape(row_count, 2, feature).astype(jnp.float32)
@@ -179,7 +173,7 @@
         P("fsdp", "expert", None),
     )
     return jax.shard_map(
-        on_device,
+        body,
         mesh=mesh,
         in_specs=placed,
         out_specs=(

time: 213 us -> 221 us (1.038)
  between operations: 1.77 us -> 15 us
  waiting for transfers between devices: 48.8 us -> 58.4 us
  other arithmetic: 29.5 us -> 20.2 us
  starting transfers between devices: 96.4 us -> 90.4 us
    ppermute x12 -> x6, starting transfers between devices: 38 us -> 20.8 us  [axis_gather(): lax.ppermute(piece, 'fsdp', shift_pairs(count, rows, cols, s, along_cols))]
    all_gather x0 -> x1, waiting for transfers between devices: none -> 16.6 us  [body(): full_in = lax.all_gather(weight_in, 'fsdp', axis=0, tiled=True)]
    all_to_all x2, waiting for transfers between devices: 14.1 us -> 0.01 us  [the longest x1 0.01 us: body(): lax.all_to_all(send, 'expert', split_axis=0, concat_axis=0, tiled=True)]
    ppermute x12 -> x6, waiting for transfers between devices: 15.5 us -> 27.4 us  [axis_gather(): lax.ppermute(piece, 'fsdp', shift_pairs(count, rows, cols, s, along_cols))]
    another operation x7 -> x3, other arithmetic: 14.6 us -> 5.28 us  [pick(): return jnp.stack(out)]
    all_to_all x2, starting transfers between devices: 22.3 us -> 31.3 us  [the longest x1 16.7 us: body(): lax.all_to_all(send, 'expert', split_axis=0, concat_axis=0, tiled=True)]
    ppermute x3, starting transfers between devices: 12.5 us -> 8.92 us  [grid_reduce_scatter(): got = lax.ppermute(part, 'fsdp', shift_pairs(count, rows, cols, s, False))]
    ppermute x3, starting transfers between devices: 8.41 us -> 11.6 us  [grid_reduce_scatter(): lax.ppermute(part, 'fsdp', shift_pairs(count, rows, cols, s, False))]
  transfers between devices with their start and end apart: 26 -> 21, of which waited for: 10 -> 9; matrix products, arithmetic and copies ran while one was open for 24% -> 12% of each run, Pallas kernels for 0% -> 0%
where the time goes in v3:
time: 221 us; the launch traced here: 217 us
  starting transfers between devices  90.4 us (41%)
  waiting for transfers between devices  58.4 us (26%)
  local copies, waits for them, and re-layouts  22.6 us (10%)
  other arithmetic  20.2 us (9%)
  between operations  15 us (7%)
  matrix products  9.92 us (4%)
    ppermute x6, waiting for transfers between devices, axis_gather(): lax.ppermute(piece, 'fsdp', shift_pairs(count, rows, cols, s, along_cols))  27.4 us
    ppermute x6, starting transfers between devices, axis_gather(): lax.ppermute(piece, 'fsdp', shift_pairs(count, rows, cols, s, along_cols))  20.8 us
    all_to_all x1, starting transfers between devices, body(): lax.all_to_all(send, 'expert', split_axis=0, concat_axis=0, tiled=True)  16.7 us
    all_gather x1, waiting for transfers between devices, body(): full_in = lax.all_gather(weight_in, 'fsdp', axis=0, tiled=True)  16.6 us
    all_to_all x1, starting transfers between devices, body(): lax.all_to_all(back, 'expert', split_axis=0, concat_axis=0, tiled=True)  14.6 us
    ppermute x3, starting transfers between devices, grid_reduce_scatter(): lax.ppermute(part, 'fsdp', shift_pairs(count, rows, cols, s, False))  11.6 us
    ppermute x3, starting transfers between devices, grid_reduce_scatter(): got = lax.ppermute(part, 'fsdp', shift_pairs(count, rows, cols, s, True))  9.02 us
    ppermute x3, starting transfers between devices, grid_reduce_scatter(): got = lax.ppermute(part, 'fsdp', shift_pairs(count, rows, cols, s, False))  8.92 us
  transfers between devices with their start and end apart: 21, of which 9 were waited for; matrix products, arithmetic and copies ran while one was open for 12% of the time, Pallas kernels for 0%

profile of v3, /device:TPU:1, one launch (start us, length us, event | category | flops | bytes accessed | tf_op | source)
XLA Modules:
  0.0 216.6 jit_solution(4871742642847532079)
XLA Ops:
  19.3 16.7 %all-to-all-start = ((bf16[64,16,512]{2,1,0:T(8,128)(2,1)}), bf16[64,16,512]{2,1,0:T(8,128)(2,1)S(1)}, u32[]{:S(2)}, u32[]{:S(2)}) async-start(bf16[64,16,512]{2,1,0:T(8,128)(2,1)} %pad_maximum_fusion), calls=%async_computation | async-start | bytes 2097152 | tf_op jit(solution)/shard_map/all_to_all | solution.py:123
  36.8 4.8 %collective-permute-start.1 = (bf16[64,2,512]{2,1,0:T(2,128)(2,1)S(1)}, bf16[64,2,512]{2,1,0:T(2,128)(2,1)S(1)}, u32[]{:S(2)}, u32[]{:S(2)}) collective-permute-start(bf16[64,2,512]{2,1,0:T(2,128)(2,1)S(1)} %copy-done.7), channel_id=1, source_target_pairs={{0,8},{1,9},{2,10},{3,11},{4,12},{5,13},{6,14},{7,15},{8,0},{9,1},... | collective-permute-start | bytes 393224 | tf_op jit(solution)/shard_map/ppermute | solution.py:52
  44.0 4.2 %collective-permute-start.2 = (bf16[64,2,512]{2,1,0:T(2,128)(2,1)S(1)}, bf16[64,2,512]{2,1,0:T(2,128)(2,1)S(1)}, u32[]{:S(2)}, u32[]{:S(2)}) collective-permute-start(bf16[64,2,512]{2,1,0:T(2,128)(2,1)S(1)} %copy-done.7), channel_id=1, source_target_pairs={{0,12},{1,13},{2,14},{3,15},{4,0},{5,1},{6,2},{7,3},{8,4},{9,5},{1... | collective-permute-start | bytes 393224 | tf_op jit(solution)/shard_map/ppermute | solution.py:52
  52.5 4.4 %collective-permute-start.5 = (bf16[4,64,2,512]{3,2,1,0:T(2,128)(2,1)}, bf16[4,64,2,512]{3,2,1,0:T(2,128)(2,1)S(1)}, u32[]{:S(2)}, u32[]{:S(2)}) collective-permute-start(bf16[4,64,2,512]{3,2,1,0:T(2,128)(2,1)} %pad_maximum_fusion.2), channel_id=1, source_target_pairs={{0,3},{1,0},{2,1},{3,2},{4,7},{5,4},{6,5},{7,6},{8,11},{9,8},{10,9... | collective-permute-start | bytes 1572872 | tf_op jit(solution)/shard_map/ppermute | solution.py:52
  59.3 2.7 %collective-permute-start.3 = (bf16[4,64,2,512]{3,2,1,0:T(2,128)(2,1)}, bf16[4,64,2,512]{3,2,1,0:T(2,128)(2,1)S(1)}, u32[]{:S(2)}, u32[]{:S(2)}) collective-permute-start(bf16[4,64,2,512]{3,2,1,0:T(2,128)(2,1)} %pad_maximum_fusion.2), channel_id=1, source_target_pairs={{0,1},{1,2},{2,3},{3,0},{4,5},{5,6},{6,7},{7,4},{8,9},{9,10},{10,1... | collective-permute-start | bytes 1572872 | tf_op jit(solution)/shard_map/ppermute | solution.py:52
  62.2 6.9 %collective-permute-done.5 = bf16[4,64,2,512]{3,2,1,0:T(2,128)(2,1)S(1)} collective-permute-done((bf16[4,64,2,512]{3,2,1,0:T(2,128)(2,1)}, bf16[4,64,2,512]{3,2,1,0:T(2,128)(2,1)S(1)}, u32[]{:S(2)}, u32[]{:S(2)}) %collective-permute-start.5) | collective-permute-done | bytes 524320 | tf_op jit(solution)/shard_map/ppermute | solution.py:52
  69.0 5.4 %collective-permute-done.4 = bf16[4,64,2,512]{3,2,1,0:T(2,128)(2,1)S(1)} collective-permute-done((bf16[4,64,2,512]{3,2,1,0:T(2,128)(2,1)}, bf16[4,64,2,512]{3,2,1,0:T(2,128)(2,1)S(1)}, u32[]{:S(2)}, u32[]{:S(2)}) %collective-permute-start.4) | collective-permute-done | bytes 524320 | tf_op jit(solution)/shard_map/ppermute | solution.py:52
  74.5 13.2 %collective-permute-done.3 = bf16[4,64,2,512]{3,2,1,0:T(2,128)(2,1)S(1)} collective-permute-done((bf16[4,64,2,512]{3,2,1,0:T(2,128)(2,1)}, bf16[4,64,2,512]{3,2,1,0:T(2,128)(2,1)S(1)}, u32[]{:S(2)}, u32[]{:S(2)}) %collective-permute-start.3) | collective-permute-done | bytes 524320 | tf_op jit(solution)/shard_map/ppermute | solution.py:52
  87.7 2.9 %fusion.25 = (bf16[1,4,64,2,512]{4,3,2,1,0:T(2,128)(2,1)S(1)}, bf16[1,4,64,2,512]{4,3,2,1,0:T(2,128)(2,1)S(1)}, bf16[1,4,64,2,512]{4,3,2,1,0:T(2,128)(2,1)S(1)}, bf16[1,4,64,2,512]{4,3,2,1,0:T(2,128)(2,1)S(1)}) fusion(pred[]{:T(512)S(6)} %eq.140, bf16[4,64,2,512]{3,2,1,0:T(2,128)(2,1)S(1)} %collective-permute-done.3, pred[]{:T(512)S(6)} %eq.153, ...), kind=kLoop, calls=%fused_computation.50 | loop fusion | flops 3932160 | bytes 4194316 | tf_op jit(solution)/shard_map/stack | solution.py:44
  90.6 3.9 %maximum_bitcast_fusion = bf16[4,4,64,2,512]{4,3,2,0,1:T(2,128)(2,1)S(1)} fusion(bf16[1,4,64,2,512]{4,3,2,1,0:T(2,128)(2,1)S(1)} %get-tuple-element.18, bf16[1,4,64,2,512]{4,3,2,1,0:T(2,128)(2,1)S(1)} %get-tuple-element.19, bf16[1,4,64,2,512]{4,3,2,1,0:T(2,128)(2,1)S(1)} %get-tuple-element.20, bf16[1,4,64,2,512]{4,3,2,1,0:T(2,128)(2,1)S(1)} %get-tuple-element.17), kind=kLoop, calls=%fused_computation.7 | loop fusion | flops 3145728 | bytes 4194304 | tf_op jit(solution)/shard_map/transpose | solution.py:62
  96.1 16.6 %all-gather.2.cloned.1.call-done = bf16[512,2,1024]{2,0,1:T(8,128)(2,1)} async-done(((bf16[32,2,1024]{2,0,1:T(8,128)(2,1)}), bf16[512,2,1024]{2,0,1:T(8,128)(2,1)}) %all-gather.2.cloned.1.call-update) | async-done | bytes 2097168 | tf_op jit(solution)/shard_map/all_gather | solution.py:124
  112.6 2.6 %fusion.8 = (bf16[32,2,8,1024]{3,2,0,1:T(8,128)(2,1)S(1)}, f32[2,32,8,1024]{3,2,1,0:T(8,128)S(1)}) fusion(bf16[512,2,1024]{2,0,1:T(8,128)(2,1)} %all-gather.2.cloned.1.call-done, bf16[32,2,8,512]{3,2,1,0:T(8,128)(2,1)} %get-tuple-element.29), kind=kOutput, calls=%fused_computation.20 | convolution fusion | flops 539492352 | bytes 5767168 | tf_op jit(solution)/shard_map/secd,deh->sech/dot_general | solution.py:132
  121.7 14.6 %all-to-all-start.1 = ((bf16[64,16,512]{2,1,0:T(8,128)(2,1)}), bf16[64,16,512]{2,1,0:T(8,128)(2,1)S(1)}, u32[]{:S(2)}, u32[]{:S(2)}) async-start(bf16[64,16,512]{2,1,0:T(8,128)(2,1)} %bitcast.27), calls=%async_computation.1 | async-start | bytes 2097152 | tf_op jit(solution)/shard_map/all_to_all | solution.py:147
  138.3 2.9 %copy.77 = bf16[1024,2,512]{2,0,1:T(8,128)(2,1)S(1)} copy(bf16[1024,2,512]{0,2,1:T(8,128)(2,1)} %fusion.11) | data formatting | bytes 4194304 | tf_op jit(solution)/shard_map/convert_element_type | solution.py:136
  142.4 2.8 %collective-permute-start.12 = (bf16[4,64,2,512]{3,1,0,2:T(8,128)(2,1)}, bf16[4,64,2,512]{3,1,0,2:T(8,128)(2,1)}, u32[]{:S(2)}, u32[]{:S(2)}) collective-permute-start(bf16[4,64,2,512]{3,1,0,2:T(8,128)(2,1)} %get-tuple-element.11), channel_id=1, source_target_pairs={{0,1},{1,2},{2,3},{3,0},{4,5},{5,6},{6,7},{7,4},{8,9},{9,10},{10,1... | collective-permute-start | bytes 1572872 | tf_op jit(solution)/shard_map/ppermute | solution.py:83
  145.3 3.7 %collective-permute-start.14 = (bf16[4,64,2,512]{3,1,0,2:T(8,128)(2,1)}, bf16[4,64,2,512]{3,1,0,2:T(8,128)(2,1)S(1)}, u32[]{:S(2)}, u32[]{:S(2)}) collective-permute-start(bf16[4,64,2,512]{3,1,0,2:T(8,128)(2,1)} %get-tuple-element.12), channel_id=1, source_target_pairs={{0,3},{1,0},{2,1},{3,2},{4,7},{5,4},{6,5},{7,6},{8,11},{9,8},{10,9... | collective-permute-start | bytes 1572872 | tf_op jit(solution)/shard_map/ppermute | solution.py:83
  149.0 2.5 %collective-permute-start.13 = (bf16[4,64,2,512]{3,1,0,2:T(8,128)(2,1)}, bf16[4,64,2,512]{3,1,0,2:T(8,128)(2,1)S(1)}, u32[]{:S(2)}, u32[]{:S(2)}) collective-permute-start(bf16[4,64,2,512]{3,1,0,2:T(8,128)(2,1)} %get-tuple-element.13), channel_id=1, source_target_pairs={{0,2},{1,3},{2,0},{3,1},{4,6},{5,7},{6,4},{7,5},{8,10},{9,11},{10,... | collective-permute-start | bytes 1572872 | tf_op jit(solution)/shard_map/ppermute | solution.py:83
  156.0 4.3 %collective-permute-start.8 = (bf16[4,32,2,1024]{3,1,0,2:T(8,128)(2,1)S(1)}, bf16[4,32,2,1024]{3,1,0,2:T(8,128)(2,1)S(1)}, u32[]{:S(2)}, u32[]{:S(2)}) collective-permute-start(bf16[4,32,2,1024]{3,1,0,2:T(8,128)(2,1)S(1)} %get-tuple-element.15), channel_id=1, source_target_pairs={{0,12},{1,13},{2,14},{3,15},{4,0},{5,1},{6,2},{7,3},{8,4},{9,5},{1... | collective-permute-start | bytes 1572872 | tf_op jit(solution)/shard_map/ppermute | solution.py:73
  162.8 8.0 %collective-permute-done.13 = bf16[4,64,2,512]{3,1,0,2:T(8,128)(2,1)S(1)} collective-permute-done((bf16[4,64,2,512]{3,1,0,2:T(8,128)(2,1)}, bf16[4,64,2,512]{3,1,0,2:T(8,128)(2,1)S(1)}, u32[]{:S(2)}, u32[]{:S(2)}) %collective-permute-start.13) | collective-permute-done | bytes 524320 | tf_op jit(solution)/shard_map/ppermute | solution.py:83
  172.2 6.0 %collective-permute-start.15 = (f32[64,2,512]{2,0,1:T(8,128)S(1)}, f32[64,2,512]{2,0,1:T(8,128)S(1)}, u32[]{:S(2)}, u32[]{:S(2)}) collective-permute-start(f32[64,2,512]{2,0,1:T(8,128)S(1)} %get-tuple-element.21), channel_id=1, source_target_pairs={{0,4},{1,5},{2,6},{3,7},{4,8},{5,9},{6,10},{7,11},{8,12},{9,13},{1... | collective-permute-start | bytes 786440 | tf_op jit(solution)/shard_map/ppermute | solution.py:88
  180.2 3.7 %collective-permute-start.16 = (f32[64,2,512]{2,0,1:T(8,128)S(1)}, f32[64,2,512]{2,0,1:T(8,128)S(1)}, u32[]{:S(2)}, u32[]{:S(2)}) collective-permute-start(f32[64,2,512]{2,0,1:T(8,128)S(1)} %get-tuple-element.23), channel_id=1, source_target_pairs={{0,8},{1,9},{2,10},{3,11},{4,12},{5,13},{6,14},{7,15},{8,0},{9,1},... | collective-permute-start | bytes 786440 | tf_op jit(solution)/shard_map/ppermute | solution.py:88
  186.9 4.3 %collective-permute-start.10 = (f32[32,2,1024]{2,1,0:T(2,128)S(1)}, f32[32,2,1024]{2,1,0:T(2,128)}, u32[]{:S(2)}, u32[]{:S(2)}) collective-permute-start(f32[32,2,1024]{2,1,0:T(2,128)S(1)} %bitcast.174), channel_id=1, source_target_pairs={{0,2},{1,3},{2,0},{3,1},{4,6},{5,7},{6,4},{7,5},{8,10},{9,11},{10,... | collective-permute-start | bytes 786440 | tf_op jit(solution)/shard_map/ppermute | solution.py:78
  195.6 3.6 %collective-permute-done.10 = f32[32,2,1024]{2,1,0:T(2,128)} collective-permute-done((f32[32,2,1024]{2,1,0:T(2,128)S(1)}, f32[32,2,1024]{2,1,0:T(2,128)}, u32[]{:S(2)}, u32[]{:S(2)}) %collective-permute-start.10) | collective-permute-done | bytes 262176 | tf_op jit(solution)/shard_map/ppermute | solution.py:78
  199.3 2.8 %collective-permute-done.11 = f32[32,2,1024]{2,1,0:T(2,128)} collective-permute-done((f32[32,2,1024]{2,1,0:T(2,128)S(1)}, f32[32,2,1024]{2,1,0:T(2,128)}, u32[]{:S(2)}, u32[]{:S(2)}) %collective-permute-start.11) | collective-permute-done | bytes 262176 | tf_op jit(solution)/shard_map/ppermute | solution.py:78
  (110 shorter events, 58.1 us)
Async XLA Ops:
  18.1 18.0 %copy-start.5 = (bf16[32,2,1024]{2,1,0:T(2,128)(2,1)S(1)}, bf16[32,2,1024]{2,1,0:T(2,128)(2,1)}, u32[]{:S(2)}) copy-start(bf16[32,2,1024]{2,1,0:T(2,128)(2,1)} %param.12) | copy-start | bytes 393220
  18.2 18.7 %copy-start.7 = (bf16[64,2,512]{2,1,0:T(2,128)(2,1)S(1)}, bf16[64,2,512]{2,1,0:T(2,128)(2,1)}, u32[]{:S(2)}) copy-start(bf16[64,2,512]{2,1,0:T(2,128)(2,1)} %param.13) | copy-start | bytes 393220
  19.3 75.6 %all-to-all-start = ((bf16[64,16,512]{2,1,0:T(8,128)(2,1)}), bf16[64,16,512]{2,1,0:T(8,128)(2,1)S(1)}, u32[]{:S(2)}, u32[]{:S(2)}) async-start(bf16[64,16,512]{2,1,0:T(8,128)(2,1)} %pad_maximum_fusion), calls=%async_computation | async-start | bytes 2097152 | tf_op jit(solution)/shard_map/all_to_all | solution.py:123
  36.1 76.6 %all-gather.2.cloned.1.call-start = ((), (), s32[]{:S(2)}) async-start(), calls=%async_computation.2 | async-start | bytes 2228224 | tf_op jit(solution)/shard_map/all_gather | solution.py:124
  36.8 11.4 %collective-permute-start.1 = (bf16[64,2,512]{2,1,0:T(2,128)(2,1)S(1)}, bf16[64,2,512]{2,1,0:T(2,128)(2,1)S(1)}, u32[]{:S(2)}, u32[]{:S(2)}) collective-permute-start(bf16[64,2,512]{2,1,0:T(2,128)(2,1)S(1)} %copy-done.7), channel_id=1, source_target_pairs={{0,8},{1,9},{2,10},{3,11},{4,12},{5,13},{6,14},{7,15},{8,0},{9,1},... | collective-permute-start | bytes 393224 | tf_op jit(solution)/shard_map/ppermute | solution.py:52
  41.7 7.6 %collective-permute-start = (bf16[64,2,512]{2,1,0:T(2,128)(2,1)S(1)}, bf16[64,2,512]{2,1,0:T(2,128)(2,1)S(1)}, u32[]{:S(2)}, u32[]{:S(2)}) collective-permute-start(bf16[64,2,512]{2,1,0:T(2,128)(2,1)S(1)} %copy-done.7), channel_id=1, source_target_pairs={{0,4},{1,5},{2,6},{3,7},{4,8},{5,9},{6,10},{7,11},{8,12},{9,13},{1... | collective-permute-start | bytes 393224 | tf_op jit(solution)/shard_map/ppermute | solution.py:52
  44.0 6.1 %collective-permute-start.2 = (bf16[64,2,512]{2,1,0:T(2,128)(2,1)S(1)}, bf16[64,2,512]{2,1,0:T(2,128)(2,1)S(1)}, u32[]{:S(2)}, u32[]{:S(2)}) collective-permute-start(bf16[64,2,512]{2,1,0:T(2,128)(2,1)S(1)} %copy-done.7), channel_id=1, source_target_pairs={{0,12},{1,13},{2,14},{3,15},{4,0},{5,1},{6,2},{7,3},{8,4},{9,5},{1... | collective-permute-start | bytes 393224 | tf_op jit(solution)/shard_map/ppermute | solution.py:52
  52.5 16.5 %collective-permute-start.5 = (bf16[4,64,2,512]{3,2,1,0:T(2,128)(2,1)}, bf16[4,64,2,512]{3,2,1,0:T(2,128)(2,1)S(1)}, u32[]{:S(2)}, u32[]{:S(2)}) collective-permute-start(bf16[4,64,2,512]{3,2,1,0:T(2,128)(2,1)} %pad_maximum_fusion.2), channel_id=1, source_target_pairs={{0,3},{1,0},{2,1},{3,2},{4,7},{5,4},{6,5},{7,6},{8,11},{9,8},{10,9... | collective-permute-start | bytes 1572872 | tf_op jit(solution)/shard_map/ppermute | solution.py:52
  56.9 17.6 %collective-permute-start.4 = (bf16[4,64,2,512]{3,2,1,0:T(2,128)(2,1)}, bf16[4,64,2,512]{3,2,1,0:T(2,128)(2,1)S(1)}, u32[]{:S(2)}, u32[]{:S(2)}) collective-permute-start(bf16[4,64,2,512]{3,2,1,0:T(2,128)(2,1)} %pad_maximum_fusion.2), channel_id=1, source_target_pairs={{0,2},{1,3},{2,0},{3,1},{4,6},{5,7},{6,4},{7,5},{8,10},{9,11},{10,... | collective-permute-start | bytes 1572872 | tf_op jit(solution)/shard_map/ppermute | solution.py:52
  59.3 28.3 %collective-permute-start.3 = (bf16[4,64,2,512]{3,2,1,0:T(2,128)(2,1)}, bf16[4,64,2,512]{3,2,1,0:T(2,128)(2,1)S(1)}, u32[]{:S(2)}, u32[]{:S(2)}) collective-permute-start(bf16[4,64,2,512]{3,2,1,0:T(2,128)(2,1)} %pad_maximum_fusion.2), channel_id=1, source_target_pairs={{0,1},{1,2},{2,3},{3,0},{4,5},{5,6},{6,7},{7,4},{8,9},{9,10},{10,1... | collective-permute-start | bytes 1572872 | tf_op jit(solution)/shard_map/ppermute | solution.py:52
  120.1 16.2 %copy-start.3 = (bf16[32,2,8,512]{3,2,1,0:T(8,128)(2,1)S(1)}, bf16[32,2,8,512]{3,2,1,0:T(8,128)(2,1)}, u32[]{:S(2)}) copy-start(bf16[32,2,8,512]{3,2,1,0:T(8,128)(2,1)} %get-tuple-element.28) | copy-start | bytes 1572868
  121.7 82.6 %all-to-all-start.1 = ((bf16[64,16,512]{2,1,0:T(8,128)(2,1)}), bf16[64,16,512]{2,1,0:T(8,128)(2,1)S(1)}, u32[]{:S(2)}, u32[]{:S(2)}) async-start(bf16[64,16,512]{2,1,0:T(8,128)(2,1)} %bitcast.27), calls=%async_computation.1 | async-start | bytes 2097152 | tf_op jit(solution)/shard_map/all_to_all | solution.py:147
  142.4 18.0 %collective-permute-start.12 = (bf16[4,64,2,512]{3,1,0,2:T(8,128)(2,1)}, bf16[4,64,2,512]{3,1,0,2:T(8,128)(2,1)}, u32[]{:S(2)}, u32[]{:S(2)}) collective-permute-start(bf16[4,64,2,512]{3,1,0,2:T(8,128)(2,1)} %get-tuple-element.11), channel_id=1, source_target_pairs={{0,1},{1,2},{2,3},{3,0},{4,5},{5,6},{6,7},{7,4},{8,9},{9,10},{10,1... | collective-permute-start | bytes 1572872 | tf_op jit(solution)/shard_map/ppermute | solution.py:83
  145.3 17.5 %collective-permute-start.14 = (bf16[4,64,2,512]{3,1,0,2:T(8,128)(2,1)}, bf16[4,64,2,512]{3,1,0,2:T(8,128)(2,1)S(1)}, u32[]{:S(2)}, u32[]{:S(2)}) collective-permute-start(bf16[4,64,2,512]{3,1,0,2:T(8,128)(2,1)} %get-tuple-element.12), channel_id=1, source_target_pairs={{0,3},{1,0},{2,1},{3,2},{4,7},{5,4},{6,5},{7,6},{8,11},{9,8},{10,9... | collective-permute-start | bytes 1572872 | tf_op jit(solution)/shard_map/ppermute | solution.py:83
  149.0 21.8 %collective-permute-start.13 = (bf16[4,64,2,512]{3,1,0,2:T(8,128)(2,1)}, bf16[4,64,2,512]{3,1,0,2:T(8,128)(2,1)S(1)}, u32[]{:S(2)}, u32[]{:S(2)}) collective-permute-start(bf16[4,64,2,512]{3,1,0,2:T(8,128)(2,1)} %get-tuple-element.13), channel_id=1, source_target_pairs={{0,2},{1,3},{2,0},{3,1},{4,6},{5,7},{6,4},{7,5},{8,10},{9,11},{10,... | collective-permute-start | bytes 1572872 | tf_op jit(solution)/shard_map/ppermute | solution.py:83
  153.8 26.3 %collective-permute-start.6 = (bf16[4,32,2,1024]{3,1,0,2:T(8,128)(2,1)S(1)}, bf16[4,32,2,1024]{3,1,0,2:T(8,128)(2,1)S(1)}, u32[]{:S(2)}, u32[]{:S(2)}) collective-permute-start(bf16[4,32,2,1024]{3,1,0,2:T(8,128)(2,1)S(1)} %get-tuple-element.14), channel_id=1, source_target_pairs={{0,4},{1,5},{2,6},{3,7},{4,8},{5,9},{6,10},{7,11},{8,12},{9,13},{1... | collective-permute-start | bytes 1572872 | tf_op jit(solution)/shard_map/ppermute | solution.py:73
  156.0 27.8 %collective-permute-start.8 = (bf16[4,32,2,1024]{3,1,0,2:T(8,128)(2,1)S(1)}, bf16[4,32,2,1024]{3,1,0,2:T(8,128)(2,1)S(1)}, u32[]{:S(2)}, u32[]{:S(2)}) collective-permute-start(bf16[4,32,2,1024]{3,1,0,2:T(8,128)(2,1)S(1)} %get-tuple-element.15), channel_id=1, source_target_pairs={{0,12},{1,13},{2,14},{3,15},{4,0},{5,1},{6,2},{7,3},{8,4},{9,5},{1... | collective-permute-start | bytes 1572872 | tf_op jit(solution)/shard_map/ppermute | solution.py:73
  160.4 23.5 %collective-permute-start.7 = (bf16[4,32,2,1024]{3,1,0,2:T(8,128)(2,1)S(1)}, bf16[4,32,2,1024]{3,1,0,2:T(8,128)(2,1)S(1)}, u32[]{:S(2)}, u32[]{:S(2)}) collective-permute-start(bf16[4,32,2,1024]{3,1,0,2:T(8,128)(2,1)S(1)} %get-tuple-element.16), channel_id=1, source_target_pairs={{0,8},{1,9},{2,10},{3,11},{4,12},{5,13},{6,14},{7,15},{8,0},{9,1},... | collective-permute-start | bytes 1572872 | tf_op jit(solution)/shard_map/ppermute | solution.py:73
  172.2 19.0 %collective-permute-start.15 = (f32[64,2,512]{2,0,1:T(8,128)S(1)}, f32[64,2,512]{2,0,1:T(8,128)S(1)}, u32[]{:S(2)}, u32[]{:S(2)}) collective-permute-start(f32[64,2,512]{2,0,1:T(8,128)S(1)} %get-tuple-element.21), channel_id=1, source_target_pairs={{0,4},{1,5},{2,6},{3,7},{4,8},{5,9},{6,10},{7,11},{8,12},{9,13},{1... | collective-permute-start | bytes 786440 | tf_op jit(solution)/shard_map/ppermute | solution.py:88
  178.2 15.6 %collective-permute-start.17 = (f32[64,2,512]{2,0,1:T(8,128)S(1)}, f32[64,2,512]{2,0,1:T(8,128)S(1)}, u32[]{:S(2)}, u32[]{:S(2)}) collective-permute-start(f32[64,2,512]{2,0,1:T(8,128)S(1)} %get-tuple-element.22), channel_id=1, source_target_pairs={{0,12},{1,13},{2,14},{3,15},{4,0},{5,1},{6,2},{7,3},{8,4},{9,5},{1... | collective-permute-start | bytes 786440 | tf_op jit(solution)/shard_map/ppermute | solution.py:88
  180.2 13.6 %collective-permute-start.16 = (f32[64,2,512]{2,0,1:T(8,128)S(1)}, f32[64,2,512]{2,0,1:T(8,128)S(1)}, u32[]{:S(2)}, u32[]{:S(2)}) collective-permute-start(f32[64,2,512]{2,0,1:T(8,128)S(1)} %get-tuple-element.23), channel_id=1, source_target_pairs={{0,8},{1,9},{2,10},{3,11},{4,12},{5,13},{6,14},{7,15},{8,0},{9,1},... | collective-permute-start | bytes 786440 | tf_op jit(solution)/shard_map/ppermute | solution.py:88
  185.0 10.7 %collective-permute-start.9 = (f32[32,2,1024]{2,1,0:T(2,128)S(1)}, f32[32,2,1024]{2,1,0:T(2,128)}, u32[]{:S(2)}, u32[]{:S(2)}) collective-permute-start(f32[32,2,1024]{2,1,0:T(2,128)S(1)} %bitcast.175), channel_id=1, source_target_pairs={{0,1},{1,2},{2,3},{3,0},{4,5},{5,6},{6,7},{7,4},{8,9},{9,10},{10,1... | collective-permute-start | bytes 786440 | tf_op jit(solution)/shard_map/ppermute | solution.py:78
  186.9 12.3 %collective-permute-start.10 = (f32[32,2,1024]{2,1,0:T(2,128)S(1)}, f32[32,2,1024]{2,1,0:T(2,128)}, u32[]{:S(2)}, u32[]{:S(2)}) collective-permute-start(f32[32,2,1024]{2,1,0:T(2,128)S(1)} %bitcast.174), channel_id=1, source_target_pairs={{0,2},{1,3},{2,0},{3,1},{4,6},{5,7},{6,4},{7,5},{8,10},{9,11},{10,... | collective-permute-start | bytes 786440 | tf_op jit(solution)/shard_map/ppermute | solution.py:78
  191.2 10.9 %collective-permute-start.11 = (f32[32,2,1024]{2,1,0:T(2,128)S(1)}, f32[32,2,1024]{2,1,0:T(2,128)}, u32[]{:S(2)}, u32[]{:S(2)}) collective-permute-start(f32[32,2,1024]{2,1,0:T(2,128)S(1)} %bitcast.173), channel_id=1, source_target_pairs={{0,3},{1,0},{2,1},{3,2},{4,7},{5,4},{6,5},{7,6},{8,11},{9,8},{10,9... | collective-permute-start | bytes 786440 | tf_op jit(solution)/shard_map/ppermute | solution.py:78
  (9 other events, 53.3 us)
Sparse Core Ops, SparseCore 0:
  40.5 72.1 all-gather.1
